TPU v7x, 256 devices: a whole 4x4x8 slice. The times are simulated.
256 devices in a mesh: dp: 4 (over x_lo, core), ctx: 64 (over x_hi, z, y).
Axes of the slice: x: 4 (x_hi: 2, x_lo: 2; x = x_hi * 2 + x_lo), y: 4, z: 8, core: 2. Of those that a mesh axis runs over, the one named last changes fastest.
Arguments:
- inputs: bfloat16 [4, 8192, 2048], P('dp', 'ctx'), may hold values from -6 to 6
- b_proj: bfloat16 [4, 8192, 64], P('dp', 'ctx'), may hold values from -0.75 to 0.75
- c_proj: bfloat16 [4, 8192, 64], P('dp', 'ctx'), may hold values from -6 to 6
- step_sizes: float32 [4, 32, 8192], P('dp', None, 'ctx'), may hold values from 0.0001 to 0.37
- a_log: float32 [32], replicated, may hold values from -8 to -1.7
- skip_gain: float32 [32], replicated, may hold values from 0.5 to 1.5
- doc_lengths: int32 [4, 16], P('dp'), may hold values from 1 to 2048, 8192 in all within a row
- grad_out: bfloat16 [4, 8192, 2048], P('dp', 'ctx'), may hold values from -6 to 6
Outputs:
- input_grads: bfloat16 [4, 8192, 2048], P('dp', 'ctx')
- b_gradient: bfloat16 [4, 8192, 64], P('dp', 'ctx')
- c_gradient: bfloat16 [4, 8192, 64], P('dp', 'ctx')
- step_grads: float32 [4, 32, 8192], P('dp', None, 'ctx')
- alog_grads: float32 [32], replicated
- skip_grads: float32 [32], replicated
Inputs may be any that keep to these rules, and one draw needn't show every extreme that they name: `doc_lengths`: each row holds the 16 document lengths of one packed sequence, in order, summing to 8192; the longest is exactly 2048.
All inputs are finite; a program needn't handle non-finite values.
Results may differ from a plain program's by a relative error of at most 0.0012.
Values sent between devices are 32-bit elements; how exact they have to be, the bound alone decides.
A program may use at most 256 MiB of HBM per device.

v0:
```python
import jax
import jax.numpy as jnp
from jax import lax
from jax.sharding import PartitionSpec as P

GROUP = 128


very_negative = -1e30
highest = lax.Precision.HIGHEST


def prefix_2(x, axis, combine, identity, reverse):
    count, index = (lax.axis_size(axis), lax.axis_index(axis))
    everything = jax.tree.map(lambda part: lax.all_gather(part, axis), x)
    start = jax.tree.map(
        lambda part, zero: jnp.broadcast_to(jnp.asarray(zero, part.dtype), part.shape), x, identity
    )

    def step(k, before):
        at = count - 1 - k if reverse else k
        reached = at > index if reverse else at < index
        new = combine(before, jax.tree.map(lambda part: part[at], everything))
        return jax.tree.map(lambda a, b: jnp.where(reached, a, b), new, before)

    return lax.fori_loop(0, count, step, start)


def segment_ids(lengths, offset, row_count):
    starts = jnp.cumsum(lengths) - lengths
    places = offset + jnp.arange(row_count, dtype=jnp.int32)
    return jnp.sum((starts[None, :] <= places[:, None]).astype(jnp.int32), axis=1) - 1


def decay_logs(deltas, rate_log):
    return deltas * (-jnp.exp(rate_log))[:, None]


def intra_group(values, bvectors, cvectors, deltas, rate_log, segment):
    cumulated = jnp.cumsum(decay_logs(deltas, rate_log), axis=1)
    spread = cumulated[:, :, None] - cumulated[:, None, :]
    places = jnp.arange(segment.shape[0])
    allowed = (places[:, None] >= places[None, :]) & (segment[:, None] == segment[None, :])
    kernel = jnp.exp(jnp.where(allowed[None], spread, very_negative))
    scores = jnp.dot(cvectors, bvectors.T, precision=highest)
    weights = kernel * scores[None] * deltas[:, None, :]
    return jnp.einsum("hts,shp->thp", weights, values, precision=highest)


def group_cross(values, bvectors, cvectors, deltas, rate_log, segment, before, incoming):
    cumulated = jnp.cumsum(decay_logs(deltas, rate_log), axis=1)
    living = (segment == before).astype(cumulated.dtype)
    carried = jnp.exp(cumulated) * living[None, :]
    readout = (
        jnp.einsum("tn,hpn->thp", cvectors, incoming, precision=highest)
        * jnp.transpose(carried)[:, :, None]
    )
    ending = (segment == segment[-1]).astype(cumulated.dtype)
    keeping = jnp.exp(cumulated[:, -1:] - cumulated) * deltas * ending[None, :]
    weighted = values * jnp.transpose(keeping)[:, :, None]
    fresh_part = jnp.einsum("shp,sn->hpn", weighted, bvectors, precision=highest)
    return (readout, carried[:, -1][:, None, None] * incoming + fresh_part)


def intra_run(values, bvectors, cvectors, deltas, rate_log, segment):
    row_count = values.shape[0]
    group_count = row_count // GROUP
    pieces = (
        values.reshape(group_count, GROUP, values.shape[1], values.shape[2]),
        bvectors.reshape(group_count, GROUP, bvectors.shape[1]),
        cvectors.reshape(group_count, GROUP, cvectors.shape[1]),
        jnp.transpose(deltas.reshape(deltas.shape[0], group_count, GROUP), (1, 0, 2)),
        segment.reshape(group_count, GROUP),
    )

    def within(pieces_now):
        return intra_group(
            pieces_now[0], pieces_now[1], pieces_now[2], pieces_now[3], rate_log, pieces_now[4]
        )

    outcome = lax.map(jax.checkpoint(within), pieces)
    return outcome.reshape(row_count, values.shape[1], values.shape[2])


def cross_run(values, bvectors, cvectors, deltas, rate_log, segment, before, incoming):
    row_count = values.shape[0]
    group_count = row_count // GROUP
    befores = jnp.concatenate([jnp.reshape(before, (1,)), segment[GROUP - 1 :: GROUP][:-1]])
    pieces = (
        values.reshape(group_count, GROUP, values.shape[1], values.shape[2]),
        bvectors.reshape(group_count, GROUP, bvectors.shape[1]),
        cvectors.reshape(group_count, GROUP, cvectors.shape[1]),
        jnp.transpose(deltas.reshape(deltas.shape[0], group_count, GROUP), (1, 0, 2)),
        segment.reshape(group_count, GROUP),
        befores,
    )

    def advance(carried_state, pieces_now):
        readout, next_state = group_cross(
            pieces_now[0],
            pieces_now[1],
            pieces_now[2],
            pieces_now[3],
            rate_log,
            pieces_now[4],
            pieces_now[5],
            carried_state,
        )
        return (next_state, readout)

    ending_state, readout = lax.scan(jax.checkpoint(advance), incoming, pieces)
    return (readout.reshape(row_count, values.shape[1], values.shape[2]), ending_state)


def combine_pairs(earlier, later):
    return (earlier[0] * later[0], later[0][:, None, None] * earlier[1] + later[1])


def per_device(inputs, b_proj, c_proj, step_sizes, a_log, skip_gain, doc_lengths, grad_out):
    row_count = inputs.shape[1]
    head_count = a_log.shape[0]
    head_width = inputs.shape[2] // head_count
    values = inputs[0].astype(jnp.float32).reshape(row_count, head_count, head_width)
    bvectors = b_proj[0].astype(jnp.float32)
    cvectors = c_proj[0].astype(jnp.float32)
    deltas = step_sizes[0]
    lengths = doc_lengths[0]
    upstream = grad_out[0].astype(jnp.float32).reshape(row_count, head_count, head_width)
    state_width = bvectors.shape[1]
    offset = lax.axis_index("ctx") * row_count
    segment = segment_ids(lengths, offset, row_count)
    before = segment_ids(lengths, offset - 1, 1)[0]

    def local_part(value_in, bvec_in, cvec_in, delta_in, rate_in, skip_in):
        return (
            intra_run(value_in, bvec_in, cvec_in, delta_in, rate_in, segment)
            + skip_in[None, :, None] * value_in
        )

    outcome, pull_local = jax.vjp(local_part, values, bvectors, cvectors, deltas, a_log, skip_gain)
    local_grads = pull_local(upstream)
    nothing = jnp.zeros((head_count, head_width, state_width), jnp.float32)
    readout, own_states = cross_run(
        values, bvectors, cvectors, deltas, a_log, segment, before, nothing
    )
    log_decay = decay_logs(deltas, a_log)
    through = jnp.exp(jnp.sum(log_decay, axis=1)) * (segment[-1] == before).astype(jnp.float32)
    carried = (
        jnp.exp(jnp.cumsum(log_decay, axis=1)) * (segment == before).astype(jnp.float32)[None, :]
    )
    pulled = jnp.einsum(
        "thp,tn->hpn", upstream * jnp.transpose(carried)[:, :, None], cvectors, precision=highest
    )
    identity_pair = (jnp.ones((head_count,), jnp.float32), nothing)
    prefix = prefix_2((through, own_states), "ctx", combine_pairs, identity_pair, False)
    suffix = prefix_2((through, pulled), "ctx", combine_pairs, identity_pair, True)
    incoming = prefix[1]

    def cross_part(value_in, bvec_in, cvec_in, delta_in, rate_in):
        return cross_run(value_in, bvec_in, cvec_in, delta_in, rate_in, segment, before, incoming)

    outflow, pull_cross = jax.vjp(cross_part, values, bvectors, cvectors, deltas, a_log)
    cross_grads = pull_cross((upstream, suffix[1]))
    rate_grad = local_grads[4] + cross_grads[4]
    totals = lax.psum((rate_grad, local_grads[5]), ("dp", "ctx"))
    value_grads = (local_grads[0] + cross_grads[0]).reshape(row_count, head_count * head_width)
    return (
        value_grads.astype(jnp.bfloat16)[None],
        (local_grads[1] + cross_grads[1]).astype(jnp.bfloat16)[None],
        (local_grads[2] + cross_grads[2]).astype(jnp.bfloat16)[None],
        (local_grads[3] + cross_grads[3])[None],
        totals[0],
        totals[1],
    )


def solution(mesh):
    in_specs = (
        P("dp", "ctx", None),
        P("dp", "ctx", None),
        P("dp", "ctx", None),
        P("dp", None, "ctx"),
        P(),
        P(),
        P("dp", None),
        P("dp", "ctx", None),
    )
    out_specs = (
        P("dp", "ctx", None),
        P("dp", "ctx", None),
        P("dp", "ctx", None),
        P("dp", None, "ctx"),
        P(),
        P(),
    )
    return jax.shard_map(
        per_device, mesh=mesh, in_specs=in_specs, out_specs=out_specs, check_vma=False
    )
```

profile of v0, /device:TPU:1, one launch (start us, length us, event | category | flops | bytes accessed | tf_op | source)
XLA Modules:
  0.0 1448.2 jit_solution(2915126778464182989)
XLA Ops:
  14.1 1.5 copy.41
  17.0 1.6 convolution_add_fusion
  18.7 1.6 fusion.42
  22.4 164.9 %all-reduce.2 = f32[2048]{0:T(1024)S(1)} all-reduce(f32[2048]{0:T(1024)S(1)} %multiply_dynamic-update-slice_fusion), channel_id=2, replica_groups=mesh['dp'=4,'ctx'=64] {'ctx'}, use_global_device_ids=true, to_apply=%add.2 | all-reduce | flops 2048 | bytes 16384
  190.3 440.9 %all-gather.6.cloned.1.call-done = f32[2048,64,64]{2,1,0:T(8,128)} async-done(((f32[32,64,64]{2,1,0:T(8,128)}), f32[2048,64,64]{2,1,0:T(8,128)}) %all-gather.6.cloned.1.call-update) | async-done | bytes 33554448 | tf_op jit(solution)/shard_map/all_gather | solution.py:15
  631.3 97.1 %while.20 = (s32[]{:T(128)}, f32[32,64,64]{2,1,0:T(8,128)S(1)}, s32[]{:T(128)}, f32[64,32]{1,0:T(8,128)S(1)}, f32[64,32,64,64]{3,2,1,0:T(8,128)}, /*index=5*/s32[]{:T(128)}, s32[]{:T(128)}) while((s32[]{:T(128)}, f32[32,64,64]{2,1,0:T(8,128)S(1)}, s32[]{:T(128)}, f32[64,32]{1,0:T(8,128)S(1)}, f32[64,32,64,64]{3,2,1,0:T(8,128)}, ...), condition=%wide.region_7.8_spmd.clone, body=%wide.region_6.7_spmd.clone.sunk | while | flops 524292 | bytes 1573353 | solution.py:26
  644.8 1.6 fusion.67
  646.5 1.5 fusion.67
  654.0 1.5 fusion.67
  663.1 1.5 fusion.67
  664.6 1.5 fusion.67
  691.8 1.8 fusion.67
  693.6 1.6 fusion.67
  725.3 1.5 fusion.67
  728.4 512.3 %all-gather.8.cloned.1.call-done = f32[2048,64,64]{2,1,0:T(8,128)} async-done(((f32[32,64,64]{2,1,0:T(8,128)}), f32[2048,64,64]{2,1,0:T(8,128)}) %all-gather.8.cloned.1.call-update) | async-done | bytes 33554448 | tf_op jit(solution)/shard_map/all_gather | solution.py:15
  1240.7 97.2 %while.21 = (s32[]{:T(128)}, f32[32,64,64]{2,1,0:T(8,128)S(1)}, s32[]{:T(128)}, f32[64,32]{1,0:T(8,128)S(1)}, f32[64,32,64,64]{3,2,1,0:T(8,128)}, /*index=5*/s32[]{:T(128)}, s32[]{:T(128)}, s32[]{:T(128)}, s32[]{:T(128)}) while((s32[]{:T(128)}, f32[32,64,64]{2,1,0:T(8,128)S(1)}, s32[]{:T(128)}, f32[64,32]{1,0:T(8,128)S(1)}, ...), condition=%wide.region_9.10_spmd.clone, body=%wide.region_8.9_spmd.clone.sunk | while | flops 524296 | bytes 1573415 | solution.py:26
  1338.3 6.1 fusion.8
  1344.8 3.4 fusion.2
  1351.3 2.0 multiply_reduce_fusion.4
  1354.1 2.2 fusion.6
  1357.8 2.5 fusion.14
  1361.1 1.7 fusion.16
  1363.8 75.0 %all-reduce.3 = (f32[32]{0:T(128)}, f32[32]{0:T(128)}) all-reduce(f32[32]{0:T(128)S(1)} %multiply_add_fusion, f32[32]{0:T(128)S(1)} %reduce_sum.207), channel_id=1, replica_groups=mesh['dp'=4,'ctx'=64] {'dp','ctx'}, use_global_device_ids=true, to_apply=%region_23.24 | all-reduce | flops 64 | bytes 512 | tf_op jit(solution)/shard_map/psum | solution.py:165
  1438.9 2.5 fusion.13
  (329 shorter events, 196.3 us)
Async XLA Ops:
  7.2 9.1 copy-start.6
  7.2 624.1 %all-gather.6.cloned.1.call-start = ((), (), s32[]{:S(2)}) async-start(), calls=%async_computation | async-start | bytes 68157440 | tf_op jit(solution)/shard_map/all_gather | solution.py:15
  14.1 173.3 %copy-start.2 = (bf16[1,128,2048]{1,2,0:T(8,128)(2,1)}, bf16[1,128,2048]{1,2,0:T(8,128)(2,1)S(1)}, u32[]{:S(2)}) copy-start(bf16[1,128,2048]{1,2,0:T(8,128)(2,1)S(1)} %copy.40) | copy-start | bytes 1572868
  14.1 2.9 copy-start.8
  15.6 3.0 copy-start.4
  16.9 1.7 copy-start.7
  18.6 2.4 copy-start.11
  18.6 1222.1 %all-gather.8.cloned.1.call-start = ((), (), s32[]{:S(2)}) async-start(), calls=%async_computation.1 | async-start | bytes 68157440 | tf_op jit(solution)/shard_map/all_gather | solution.py:15
  20.3 169.5 %copy-start.9 = (f32[32]{0:T(128)S(1)}, f32[32]{0:T(128)}, u32[]{:S(2)}) copy-start(f32[32]{0:T(128)} %param.17) | copy-start | bytes 388
  1240.7 97.2 %copy-start.10 = (f32[32]{0:T(128)S(1)}, f32[32]{0:T(128)}, u32[]{:S(2)}) copy-start(f32[32]{0:T(128)} %param.16) | copy-start | bytes 388
  1338.3 6.5 copy-start
  1357.8 3.3 copy-start.3
  1357.8 3.3 copy-start.5
  1361.1 77.7 %copy-start.1 = (f32[128,32,64]{0,2,1:T(8,128)S(1)}, f32[128,32,64]{0,2,1:T(8,128)}, u32[]{:S(2)}) copy-start(f32[128,32,64]{0,2,1:T(8,128)} %convert.3) | copy-start | bytes 3145732
Sparse Core Ops, SparseCore 0:
  18.7 612.5 all-gather.5
  634.8 605.8 all-gather.7
where the time goes:
time: 1450 us
  waiting for transfers between devices  953 us (66%)
  blocking collectives  240 us (17%)
  other arithmetic  203 us (14%)
  matrix products  22.6 us (2%)
  between operations  16.3 us (1%)
    all_gather x2, waiting for transfers between devices, prefix_2(): everything = jax.tree.map(lambda part: lax.all_gather(part, axis), x)  953 us
    select_n x128, other arithmetic, step(): return jax.tree.map(lambda a, b: jnp.where(reached, a, b), new, before)  188 us
    unnamed x1, blocking collectives  165 us
    psum x1, blocking collectives, per_device(): totals = lax.psum((rate_grad, local_grads[5]), ('dp', 'ctx'))  75 us
  transfers between devices with their start and end apart: 2, of which 2 were waited for; matrix products, arithmetic and copies ran while one was open for 7% of the time, Pallas kernels for 0%

commit v1 on v0

v1 whole, which is shorter than its diff:
```python
import functools

import jax
import jax.numpy as jnp
from jax import lax
from jax.experimental import pallas as pl
from jax.experimental.pallas import tpu as pltpu
from jax.sharding import PartitionSpec as P

MESH = pl.DeviceIdType.MESH
f32, bf16 = jnp.float32, jnp.bfloat16

MOST_DOC = 2048
RING = 4
CHUNKS = 2


def nn(a, b):
    return lax.dot_general(a, b, (((1,), (0,)), ((), ())), preferred_element_type=f32)


def nt(a, b):
    return lax.dot_general(a, b, (((1,), (1,)), ((), ())), preferred_element_type=f32)


def split(v, count):
    pieces = []
    for i in range(count):
        piece = v.astype(bf16)
        pieces.append(piece)
        if i + 1 < count:
            v = v - piece.astype(f32)
    return pieces


def kernel(
    dims,
    x_ref, g_ref, b_ref, c_ref, dt_ref, alog_ref, skip_ref, len_ref,
    dx_ref, db_ref, dc_ref, dstep_ref, dalog_ref, dskip_ref,
    xh, gh, bd, z1, z2, rowv, vecs, sa, ra, sb, rb, sc, rc, ar,
    sa_send, sa_recv, sb_send, sb_recv, sc_send, sc_recv, ar_send, ar_recv,
):
    n_dp, n_ctx, n_z, T, H, D, N, DOCS = dims
    n_x = n_ctx // (n_z * RING)
    groups = n_ctx // RING
    rounds = -(-MOST_DOC // (RING * T))
    W = H * D // (RING * CHUNKS)
    Q = H * D // RING
    dp, me = lax.axis_index("dp"), lax.axis_index("ctx")
    y, group = me % RING, me // RING
    z, xhi = group % n_z, group // n_z

    y_peers = [(d, (y + d) % RING) for d in (2, 1, 3)]
    ahead = ((group + 1) % groups) * RING + y
    behind = ((group + groups - 1) % groups) * RING + y
    z_peers = [(xhi * n_z + (z + d) % n_z) * RING + y for d in range(1, n_z)]
    fold = dp * n_x + xhi
    f_peers = []
    for d in range(1, n_dp * n_x):
        other = (fold + d) % (n_dp * n_x)
        f_peers.append((other // n_x, ((other % n_x) * n_z + z) * RING + y))

    barrier = pltpu.get_barrier_semaphore()
    greeted = [(dp, group * RING + q) for _, q in y_peers]
    greeted += [(dp, ahead), (dp, behind)]
    greeted += [(dp, p) for p in z_peers]
    greeted += f_peers
    for target in greeted:
        pl.semaphore_signal(barrier, inc=1, device_id=target, device_id_type=MESH)

    offset = me * T
    starts, total = [], jnp.int32(0)
    for d in range(DOCS):
        starts.append(total)
        total = total + len_ref[0, d]
    rows = lax.broadcasted_iota(jnp.int32, (T, T), 0)
    cols = lax.broadcasted_iota(jnp.int32, (T, T), 1)
    lane8 = lax.broadcasted_iota(jnp.int32, (8, T), 1)
    seg_r = jnp.zeros((T, T), jnp.int32)
    seg_c = jnp.zeros((8, T), jnp.int32)
    before, last = jnp.int32(0), jnp.int32(0)
    for s in starts:
        seg_r = seg_r + jnp.where(rows + offset >= s, 1, 0)
        seg_c = seg_c + jnp.where(lane8 + offset >= s, 1, 0)
        before = before + jnp.where(s <= offset - 1, 1, 0)
        last = last + jnp.where(s <= offset + T - 1, 1, 0)
    seg_c = seg_c[0:1, :]
    same = seg_r == seg_c
    allowed = jnp.logical_and(rows >= cols, same)
    allowed_t = jnp.logical_and(cols >= rows, same)
    living_col = jnp.where(seg_r == before, 1.0, 0.0)[:, :N]
    ending_col = jnp.where(seg_r == last, 1.0, 0.0)[:, :N]
    living_row = jnp.where(seg_c == before, 1.0, 0.0)
    ending_row = jnp.where(seg_c == last, 1.0, 0.0)
    through_flag = jnp.where(last == before, 1.0, 0.0)

    tril = jnp.where(rows >= cols, 1.0, 0.0).astype(bf16)
    eye = jnp.where(rows == cols, 1.0, 0.0).astype(bf16)
    dt = dt_ref[...]
    cum_dt, dt_t = jnp.zeros((T, H), f32), jnp.zeros((T, H), f32)
    for piece in split(dt, 3):
        cum_dt = cum_dt + nt(tril, piece)
        dt_t = dt_t + nt(eye, piece)
    rate = -jnp.exp(alog_ref[...])
    cum = cum_dt * rate
    alpha = jnp.exp(cum)
    beta = jnp.exp(-cum) * dt_t
    spread = jnp.concatenate(
        [
            jnp.concatenate(split(alpha, 3), axis=1),
            jnp.concatenate(split(beta, 3), axis=1),
        ],
        axis=0,
    )
    skip3 = jnp.concatenate(split(jnp.broadcast_to(skip_ref[...], (16, H)), 3), axis=1)

    def one_hot(start, width, copies):
        heads = lax.broadcasted_iota(jnp.int32, (copies * H, width), 0) % H
        lanes = lax.broadcasted_iota(jnp.int32, (copies * H, width), 1) + start
        return jnp.where(lanes // D == heads, 1.0, 0.0).astype(bf16)

    bb, cc = b_ref[...], c_ref[...]
    b32, c32 = bb.astype(f32), cc.astype(f32)
    eye_n = eye[:N, :N]
    eb_t = (nt(eye_n, bb) * ending_row).astype(bf16)
    lc_t = (nt(eye_n, cc) * living_row).astype(bf16)
    eb_t = jnp.concatenate([eb_t, eb_t], axis=1)
    lc_t = jnp.concatenate([lc_t, lc_t], axis=1)
    eb = (b32 * ending_col).astype(bf16)
    lc = (c32 * living_col).astype(bf16)
    eb = jnp.concatenate([eb, eb], axis=1)
    lc = jnp.concatenate([lc, lc], axis=1)

    sent = []
    vecs[...] = jnp.zeros_like(vecs)
    for k in range(CHUNKS):
        for q in range(RING):
            lo = q * Q + k * W
            at = slice(lo, lo + W)
            hot = one_hot(lo, W, 3)
            wide = nn(spread, hot)
            alpha_w, beta_w = wide[:T], wide[T:]
            rowv[0:8, at] = nn(skip3, hot)[0:8]
            last_alpha = jnp.broadcast_to(alpha_w[T - 1 : T], (8, W))
            rowv[8:16, at] = last_alpha
            g = g_ref[:, at].astype(f32)
            x = x_ref[:, at].astype(f32)
            vecs[1:2, at] = jnp.sum(g * x, axis=0, keepdims=True)
            g_hi, g_lo = split(g * alpha_w, 2)
            x_hi, x_lo = split(x * beta_w, 2)
            gh[0:T, at], gh[T : 2 * T, at] = g_hi, g_lo
            xh[0:T, at], xh[T : 2 * T, at] = x_hi, x_lo
            bd[:, at] = beta_w
            sa[q, k, 0:N, :] = nn(eb_t, xh[:, at]) * last_alpha[0:1]
            sa[q, k, N : 2 * N, :] = nn(lc_t, gh[:, at])
            sa[q, k, 2 * N : 2 * N + 8, :] = last_alpha * through_flag
        if k == 0:
            pl.semaphore_wait(barrier, len(greeted))
        for _, q in y_peers:
            copy = pltpu.make_async_remote_copy(
                src_ref=sa.at[q, k],
                dst_ref=ra.at[y, k],
                send_sem=sa_send.at[q, k],
                recv_sem=sa_recv.at[y, k],
                device_id=(dp, group * RING + q),
                device_id_type=MESH,
            )
            copy.start()
            sent.append(copy)
        ra[y, k] = sa[y, k]

    s_hi, s_lo = split(jnp.where(allowed, nt(cc, bb), 0.0), 2)
    t_hi, t_lo = split(jnp.where(allowed_t, nt(bb, cc), 0.0), 2)
    s_hi = jnp.concatenate([s_hi, s_hi], axis=1)
    t_hi = jnp.concatenate([t_hi, t_hi], axis=1)
    step = 512
    both = jnp.zeros((T, 2 * T), f32)
    rest = jnp.zeros((T, T), f32)
    for lo in range(0, H * D, step):
        at = slice(lo, lo + step)
        xp, gp = xh[:, at], gh[:, at]
        z2[:, at] = nn(s_hi, xp) + nn(s_lo, xp[:T])
        z1[:, at] = nn(t_hi, gp) + nn(t_lo, gp[:T])
        both = both + nt(gp[:T], xp)
        rest = rest + nt(gp[T:], xp[:T])
    ds = jnp.where(allowed, both[:, :T] + both[:, T:] + rest, 0.0)
    dc = jnp.zeros((T, N), f32)
    for piece in split(ds, 2):
        dc = dc + nn(piece, bb)
    db = jnp.zeros((T, N), f32)
    for piece in split(ds.T, 2):
        db = db + nn(piece, cc)

    def arrived(refs, sem, index):
        pltpu.make_async_remote_copy(
            src_ref=refs, dst_ref=refs, send_sem=sem.at[index], recv_sem=sem.at[index],
            device_id=(dp, me), device_id_type=MESH,
        ).wait_recv()

    def through(r, k):
        return ra[r, k, 2 * N : 2 * N + 1, :]

    def own(r, k):
        return ra[r, k, 0:N, :]

    def pulled(r, k):
        return ra[r, k, N : 2 * N, :]

    def pass_on(r, k, up, down):
        sb[r, 0, k], sb[r, 1, k] = up, down
        for side, target in ((0, ahead), (1, behind)):
            copy = pltpu.make_async_remote_copy(
                src_ref=sb.at[r, side, k],
                dst_ref=rb.at[r, side, k],
                send_sem=sb_send.at[r, side, k],
                recv_sem=sb_recv.at[r, side, k],
                device_id=(dp, target),
                device_id_type=MESH,
            )
            copy.start()
            sent.append(copy)

    group_through, up_total, down_total = {}, {}, {}

    def event(k, r):
        if r == 0:
            for _, q in y_peers:
                arrived(ra.at[q, k], sa_recv, (q, k))
            up, down = own(0, k), pulled(RING - 1, k)
            for i in range(1, RING):
                up = own(i, k) + through(i, k) * up
                j = RING - 1 - i
                down = pulled(j, k) + through(j, k) * down
            g = through(0, k)
            for i in range(1, RING):
                g = g * through(i, k)
            group_through[k] = g
            pass_on(0, k, up, down)
            return
        for side in (0, 1):
            arrived(rb.at[r - 1, side, k], sb_recv, (r - 1, side, k))
        up, down = rb[r - 1, 0, k], rb[r - 1, 1, k]
        if r < rounds:
            pass_on(
                r, k,
                sb[0, 0, k] + group_through[k] * up,
                sb[0, 1, k] + group_through[k] * down,
            )
            return
        for i in range(RING):
            j = RING - 1 - i
            sc[i, k, 0:N, :] = up
            sc[j, k, N : 2 * N, :] = down
            if i + 1 < RING:
                up = own(i, k) + through(i, k) * up
                down = pulled(j, k) + through(j, k) * down
        for _, q in y_peers:
            copy = pltpu.make_async_remote_copy(
                src_ref=sc.at[q, k],
                dst_ref=rc.at[y, k],
                send_sem=sc_send.at[q, k],
                recv_sem=sc_recv.at[y, k],
                device_id=(dp, group * RING + q),
                device_id_type=MESH,
            )
            copy.start()
            sent.append(copy)
        rc[y, k] = sc[y, k]

    for wave in range(CHUNKS + rounds):
        for k in range(CHUNKS):
            if 0 <= wave - k <= rounds:
                event(k, wave - k)

    col_q, row_q = jnp.zeros((H, 2 * T), f32), jnp.zeros((H, 2 * T), f32)
    acc_c, acc_b = jnp.zeros((2 * T, 2 * N), f32), jnp.zeros((2 * T, 2 * N), f32)
    for k in range(CHUNKS):
        for _, q in y_peers:
            arrived(rc.at[q, k], sc_recv, (q, k))
        for q in range(RING):
            lo = q * Q + k * W
            at = slice(lo, lo + W)
            hot = one_hot(lo, W, 1)
            state, later = rc[q, k, 0:N, :], rc[q, k, N : 2 * N, :]
            last_alpha = rowv[8:9, at]
            vecs[0:1, at] = jnp.sum(
                later * (sa[q, k, 0:N, :] + last_alpha * through_flag * state),
                axis=0, keepdims=True,
            )
            hh = jnp.concatenate(split(state, 2), axis=0)
            fh = jnp.concatenate(split(later * last_alpha, 2), axis=0)
            z1_w = z1[:, at] + nn(eb, fh)
            z2_w = z2[:, at] + nn(lc, hh)
            gp, xp = gh[:, at], xh[:, at]
            p1 = z1_w * (xp[:T].astype(f32) + xp[T:].astype(f32))
            p2 = z2_w * (gp[:T].astype(f32) + gp[T:].astype(f32))
            dx_ref[:, at] = (bd[:, at] * z1_w + rowv[0:1, at] * g_ref[:, at].astype(f32)).astype(bf16)
            col_q = col_q + nt(hot, jnp.concatenate(split(p1, 2), axis=0))
            row_q = row_q + nt(hot, jnp.concatenate(split(p2, 2), axis=0))
            acc_c = acc_c + nt(gp, hh)
            acc_b = acc_b + nt(xp, fh)

    acc_c = acc_c[:T] + acc_c[T:]
    acc_b = acc_b[:T] + acc_b[T:]
    dc_ref[...] = (dc + living_col * (acc_c[:, :N] + acc_c[:, N:])).astype(bf16)
    db_ref[...] = (db + ending_col * (acc_b[:, :N] + acc_b[:, N:])).astype(bf16)

    hot = one_hot(0, H * D, 1)
    sums = jnp.zeros((H, 8), f32)
    for piece in split(vecs[...], 3):
        sums = sums + nt(hot, piece)
    col_q = col_q[:, :T] + col_q[:, T:]
    row_q = row_q[:, :T] + row_q[:, T:]
    d_log = jnp.zeros((H, T), f32) + sums[:, 0:1]
    for piece in split(row_q - col_q, 3):
        d_log = d_log + nn(piece, tril)
    head_r = lax.broadcasted_iota(jnp.int32, (H, H), 0)
    head_c = lax.broadcasted_iota(jnp.int32, (H, H), 1)
    rate_c = jnp.sum(jnp.where(head_r == head_c, jnp.broadcast_to(rate, (H, H)), 0.0), axis=1, keepdims=True)
    d_dt = d_log * rate_c
    dstep_ref[...] = col_q / dt + d_dt
    dalog = jnp.sum(d_dt * dt, axis=1, keepdims=True)
    on_diagonal = rows[:H] == cols[:H]
    alog_row = jnp.sum(jnp.where(on_diagonal, dalog, 0.0), axis=0, keepdims=True)
    skip_row = jnp.sum(jnp.where(on_diagonal, sums[:, 1:2], 0.0), axis=0, keepdims=True)
    row8 = lax.broadcasted_iota(jnp.int32, (8, T), 0)
    part = jnp.where(row8 == 0, alog_row, jnp.where(row8 == 1, skip_row, 0.0))

    stages = (
        (y, RING, [(dp, group * RING + (y + d) % RING) for d in range(1, RING)]),
        (z, n_z, [(dp, p) for p in z_peers]),
        (fold, n_dp * n_x, f_peers),
    )
    for s, (mine, count, peers) in enumerate(stages):
        ar[s, mine] = part
        for d, target in enumerate(peers, 1):
            copy = pltpu.make_async_remote_copy(
                src_ref=ar.at[s, mine],
                dst_ref=ar.at[s, mine],
                send_sem=ar_send.at[s, d],
                recv_sem=ar_recv.at[s, mine],
                device_id=target,
                device_id_type=MESH,
            )
            copy.start()
            sent.append(copy)
        for d in range(1, count):
            other = (mine + d) % count
            arrived(ar.at[s, other], ar_recv, (s, other))
        part = ar[s, 0]
        for i in range(1, count):
            part = part + ar[s, i]
    dalog_ref[...] = part[0:1, :H]
    dskip_ref[...] = part[1:2, :H]
    for copy in sent:
        copy.wait_send()


def per_device(n_dp, n_ctx, n_z, inputs, b_proj, c_proj, step_sizes, a_log, skip_gain, doc_lengths, grad_out):
    T, H, N = inputs.shape[1], a_log.shape[0], b_proj.shape[2]
    D = inputs.shape[2] // H
    HD = H * D
    K, W = CHUNKS, HD // (RING * CHUNKS)
    rounds = -(-MOST_DOC // (RING * T))
    n_x = n_ctx // (n_z * RING)
    slots = max(RING, n_z, n_dp * n_x)
    dims = (n_dp, n_ctx, n_z, T, H, D, N, doc_lengths.shape[1])
    vmem = pl.BlockSpec(memory_space=pltpu.VMEM)
    dma = pltpu.SemaphoreType.DMA
    dx, db, dc, dstep, dalog, dskip = pl.pallas_call(
        functools.partial(kernel, dims),
        out_shape=(
            jax.ShapeDtypeStruct((T, HD), bf16),
            jax.ShapeDtypeStruct((T, N), bf16),
            jax.ShapeDtypeStruct((T, N), bf16),
            jax.ShapeDtypeStruct((H, T), f32),
            jax.ShapeDtypeStruct((1, H), f32),
            jax.ShapeDtypeStruct((1, H), f32),
        ),
        in_specs=[vmem] * 7 + [pl.BlockSpec(memory_space=pltpu.SMEM)],
        out_specs=(vmem,) * 6,
        scratch_shapes=[
            pltpu.VMEM((2 * T, HD), bf16),
            pltpu.VMEM((2 * T, HD), bf16),
            pltpu.VMEM((T, HD), f32),
            pltpu.VMEM((T, HD), f32),
            pltpu.VMEM((T, HD), f32),
            pltpu.VMEM((16, HD), f32),
            pltpu.VMEM((8, HD), f32),
            pltpu.VMEM((RING, K, 2 * N + 8, W), f32),
            pltpu.VMEM((RING, K, 2 * N + 8, W), f32),
            pltpu.VMEM((rounds, 2, K, N, W), f32),
            pltpu.VMEM((rounds, 2, K, N, W), f32),
            pltpu.VMEM((RING, K, 2 * N, W), f32),
            pltpu.VMEM((RING, K, 2 * N, W), f32),
            pltpu.VMEM((3, slots, 8, 128), f32),
            dma((RING, K)),
            dma((RING, K)),
            dma((rounds, 2, K)),
            dma((rounds, 2, K)),
            dma((RING, K)),
            dma((RING, K)),
            dma((3, slots)),
            dma((3, slots)),
        ],
        compiler_params=pltpu.CompilerParams(
            collective_id=0, has_side_effects=True, vmem_limit_bytes=40 << 20
        ),
        name="ssd_backward",
    )(
        inputs[0], grad_out[0], b_proj[0], c_proj[0], step_sizes[0],
        a_log[None], skip_gain[None], doc_lengths,
    )
    return dx[None], db[None], dc[None], dstep[None], dalog[0], dskip[0]


def solution(mesh):
    tokens, heads = P("dp", "ctx", None), P("dp", None, "ctx")
    n_dp, n_ctx = mesh.shape["dp"], mesh.shape["ctx"]
    n_z = min(8, n_ctx // RING)
    return jax.shard_map(
        functools.partial(per_device, n_dp, n_ctx, n_z),
        mesh=mesh,
        in_specs=(tokens, tokens, tokens, heads, P(), P(), P("dp", None), tokens),
        out_specs=(tokens, tokens, tokens, heads, P(), P()),
        check_vma=False,
    )
```

time: 1450 us -> 75.5 us (0.05)
  waiting for transfers between devices: 953 us -> 0 us
  blocking collectives: 240 us -> 0 us
  other arithmetic: 203 us -> 0 us
  Pallas kernels: 0 us -> 67 us
  matrix products: 22.6 us -> 0 us
  between operations: 16.3 us -> 0.7 us
    all_gather x2 -> x0, waiting for transfers between devices: 953 us -> none  [prefix_2(): everything = jax.tree.map(lambda part: lax.all_gather(part, axis), x)]
    select_n x128 -> x0, other arithmetic: 188 us -> none  [step(): return jax.tree.map(lambda a, b: jnp.where(reached, a, b), new, before)]
    unnamed x1 -> x0, blocking collectives: 165 us -> none
    psum x1 -> x0, blocking collectives: 75 us -> none  [per_device(): totals = lax.psum((rate_grad, local_grads[5]), ('dp', 'ctx'))]
    pallas_call x0 -> x1, Pallas kernels: none -> 67 us  [per_device(): pl.pallas_call(functools.partial(kernel, dims), out_shape=(jax.ShapeDtype...]
    dot_general x11 -> x0, matrix products: 22.6 us -> none  [the longest x2 9.49 us: intra_group(): return jnp.einsum('hts,shp->thp', weights, values, precision=highest)]
  transfers between devices with their start and end apart: 2 -> 0, of which waited for: 2 -> 0; matrix products, arithmetic and copies ran while one was open for 7% -> 0% of each run, Pallas kernels for 0% -> 0%
where the time goes in v1:
time: 75.5 us; the launch traced here: 75.3 us
  Pallas kernels  67 us (89%)
  local copies, waits for them, and re-layouts  7.52 us (10%)
    pallas_call x1, Pallas kernels, per_device(): pl.pallas_call(functools.partial(kernel, dims), out_shape=(jax.ShapeDtype...  67 us
    unnamed x22, local copies, waits for them, and re-layouts  7.52 us

profile of v1, /device:TPU:1, one launch (start us, length us, event | category | flops | bytes accessed | tf_op | source)
XLA Modules:
  0.0 75.3 jit_solution(7575576963989526408)
XLA Ops:
  0.6 0.0 copy-start.6
  0.6 0.8 %copy.14 = bf16[1,128,64]{2,1,0:T(8,128)(2,1)S(1)} copy(bf16[1,128,64]{1,2,0:T(8,128)(2,1)} %param.9) | data formatting | bytes 32768 | tf_op args[1]
  1.5 0.0 copy-done.6
  1.5 0.0 copy-start.2
  1.5 0.1 copy.15
  1.6 0.0 copy-start.3
  1.6 0.0 copy-start.4
  1.6 0.0 copy-start.5
  1.6 0.6 copy-done.2
  2.2 0.1 copy-done.3
  2.3 0.0 copy-done.4
  2.3 0.0 copy-done.5
  2.3 0.0 copy-start
  2.3 1.0 %copy-done = bf16[1,128,2048]{2,1,0:T(8,128)(2,1)S(1)} copy-done((bf16[1,128,2048]{2,1,0:T(8,128)(2,1)S(1)}, bf16[1,128,2048]{2,1,0:T(8,128)(2,1)}, u32[]{:S(2)}) %copy-start) | copy-done | bytes 524312
  3.4 0.0 copy-start.1
  3.4 1.0 %copy-done.1 = bf16[1,128,2048]{2,1,0:T(8,128)(2,1)S(1)} copy-done((bf16[1,128,2048]{2,1,0:T(8,128)(2,1)S(1)}, bf16[1,128,2048]{2,1,0:T(8,128)(2,1)}, u32[]{:S(2)}) %copy-start.1) | copy-done | bytes 524312
  4.4 67.0 %ssd_backward.1 = (bf16[128,2048]{1,0:T(8,128)(2,1)S(1)}, bf16[128,64]{1,0:T(8,128)(2,1)S(1)}, bf16[128,64]{1,0:T(8,128)(2,1)S(1)}, f32[32,128]{1,0:T(8,128)S(1)...) custom-call(bf16[128,2048]{1,0:T(8,128)(2,1)S(1)} %bitcast.13, bf16[128,2048]{1,0:T(8,128)(2,1)S(1)} %bitcast.14, ...), custom_call_target="tpu_custom_call" | custom-call | tf_op jit(solution)/shard_map/ssd_backward/pallas_call | solution.py:370
  71.4 0.7 copy.16
  72.1 0.7 copy.17
  72.8 0.8 %copy.22 = bf16[1,128,2048]{2,1,0:T(8,128)(2,1)} copy(bf16[1,128,2048]{2,1,0:T(8,128)(2,1)S(1)} %bitcast.15) | data formatting | bytes 1048576
  73.6 0.6 copy.23
  74.2 0.5 copy.24
  74.7 0.5 copy.25
Async XLA Ops:
  0.6 0.8 %copy-start.6 = (bf16[1,128,64]{1,2,0:T(8,128)(2,1)S(1)}, bf16[1,128,64]{1,2,0:T(8,128)(2,1)}, u32[]{:S(2)}) copy-start(bf16[1,128,64]{1,2,0:T(8,128)(2,1)} %param.10) | copy-start | bytes 49156
  1.5 0.7 copy-start.2
  1.6 0.7 copy-start.3
  1.6 0.7 copy-start.4
  1.6 0.7 copy-start.5
  2.3 1.0 %copy-start = (bf16[1,128,2048]{2,1,0:T(8,128)(2,1)S(1)}, bf16[1,128,2048]{2,1,0:T(8,128)(2,1)}, u32[]{:S(2)}) copy-start(bf16[1,128,2048]{2,1,0:T(8,128)(2,1)} %param.8) | copy-start | bytes 1572868
  3.4 1.0 %copy-start.1 = (bf16[1,128,2048]{2,1,0:T(8,128)(2,1)S(1)}, bf16[1,128,2048]{2,1,0:T(8,128)(2,1)}, u32[]{:S(2)}) copy-start(bf16[1,128,2048]{2,1,0:T(8,128)(2,1)} %param.15) | copy-start | bytes 1572868

commit v2 on v1

v2 whole, which is shorter than its diff:
```python
import functools

import jax
import jax.numpy as jnp
from jax import lax
from jax.experimental import pallas as pl
from jax.experimental.pallas import tpu as pltpu
from jax.sharding import PartitionSpec as P

MESH = pl.DeviceIdType.MESH
f32, bf16 = jnp.float32, jnp.bfloat16

MOST_DOC = 2048
RING = 4
CHUNKS = 4
ORDER = (
    ("total", 0), ("total", 1), ("pair", 0), ("total", 2), ("pair", 1), ("total", 3), ("pair", 2), ("give", 0),
    ("pair", 3), ("give", 1), ("give", 2), ("finish", 0), ("give", 3), ("finish", 1), ("finish", 2), ("finish", 3),
)


def nn(a, b):
    return lax.dot_general(a, b, (((1,), (0,)), ((), ())), preferred_element_type=f32)


def nt(a, b):
    return lax.dot_general(a, b, (((1,), (1,)), ((), ())), preferred_element_type=f32)


def split(v, count):
    pieces = []
    for i in range(count):
        piece = v.astype(bf16)
        pieces.append(piece)
        if i + 1 < count:
            v = v - piece.astype(f32)
    return pieces


def kernel(
    dims,
    x_hbm, g_hbm, bt_hbm, ct_hbm, dt_hbm, alog_hbm, skip_hbm, len_hbm,
    dx_hbm, db_hbm, dc_hbm, dstep_hbm, dalog_hbm, dskip_hbm,
    dx_ref, db_ref, dc_ref, dstep_ref, dalog_ref, dskip_ref,
    x_ref, g_ref, bt_ref, ct_ref, dt_ref, alog_ref, skip_ref, len_ref,
    xh, gh, bd, z1, z2, rowv, vecs, sa, ra, s1, r1, s2, r2, r3, sc, rc, ar,
    load, store, sa_send, sa_recv, s1_send, r1_recv, s2_send, r2_recv, s3_send, r3_recv, sc_send, sc_recv, ar_send, ar_recv,
):
    n_dp, n_ctx, n_z, T, H, D, N, DOCS = dims
    n_x = n_ctx // (n_z * RING)
    groups = n_ctx // RING
    W = H * D // (RING * CHUNKS)
    C = RING * W
    dp, me = lax.axis_index("dp"), lax.axis_index("ctx")
    y, group = me % RING, me // RING
    z, xhi = group % n_z, group // n_z

    y_peers = [(d, (y + d) % RING) for d in (2, 1, 3)]
    z_near = [(dp, ((group + d) % groups) * RING + y) for d in (1, groups - 1)]
    z_far = [(dp, ((group + d + groups) % groups) * RING + y) for d in (3, -3)]
    z_peers = [(dp, (xhi * n_z + (z + d) % n_z) * RING + y) for d in range(1, n_z)]
    fold = dp * n_x + xhi
    f_peers = []
    for d in range(1, n_dp * n_x):
        other = (fold + d) % (n_dp * n_x)
        f_peers.append((other // n_x, ((other % n_x) * n_z + z) * RING + y))

    barrier = pltpu.get_barrier_semaphore()
    greeted = [(dp, group * RING + q) for _, q in y_peers]
    greeted += z_near + z_far + z_peers + f_peers
    for target in greeted:
        pl.semaphore_signal(barrier, inc=1, device_id=target, device_id_type=MESH)

    pairs = [(len_hbm, len_ref), (dt_hbm, dt_ref), (alog_hbm, alog_ref), (bt_hbm, bt_ref), (ct_hbm, ct_ref), (skip_hbm, skip_ref)]
    small = len(pairs)
    for k in range(CHUNKS):
        at = slice(k * C, (k + 1) * C)
        pairs += [(g_hbm.at[:, at], g_ref.at[:, at]), (x_hbm.at[:, at], x_ref.at[:, at])]
    loads = [pltpu.make_async_copy(a, b, load.at[i]) for i, (a, b) in enumerate(pairs)]
    for copy in loads:
        copy.start()

    rows = lax.broadcasted_iota(jnp.int32, (T, T), 0)
    cols = lax.broadcasted_iota(jnp.int32, (T, T), 1)
    tril = jnp.where(rows >= cols, 1.0, 0.0).astype(bf16)
    eye = jnp.where(rows == cols, 1.0, 0.0).astype(bf16)
    head_r = lax.broadcasted_iota(jnp.int32, (H, H), 0)
    head_c = lax.broadcasted_iota(jnp.int32, (H, H), 1)

    def one_hot(k, copies):
        heads = lax.broadcasted_iota(jnp.int32, (copies * H, C), 0) % H
        lanes = lax.broadcasted_iota(jnp.int32, (copies * H, C), 1) + k * C
        return jnp.where(lanes // D == heads, 1.0, 0.0).astype(bf16)

    for copy in loads[:small]:
        copy.wait()

    offset = me * T
    lengths = len_ref[...]
    doc_r = lax.broadcasted_iota(jnp.int32, (DOCS, DOCS), 0)
    doc_c = lax.broadcasted_iota(jnp.int32, (DOCS, DOCS), 1)
    length_col = jnp.sum(jnp.where(doc_r == doc_c, lengths, 0), axis=1, keepdims=True)
    start_col = jnp.sum(jnp.where(doc_c < doc_r, lengths, 0), axis=1, keepdims=True)
    start_row = jnp.sum(jnp.where(doc_r < doc_c, length_col, 0), axis=0, keepdims=True)
    place_row = lax.broadcasted_iota(jnp.int32, (DOCS, T), 1) + offset
    place_col = lax.broadcasted_iota(jnp.int32, (T, DOCS), 0) + offset
    seg_row = jnp.sum(jnp.where(start_col <= place_row, 1.0, 0.0), axis=0, keepdims=True)
    seg_col = jnp.sum(jnp.where(start_row <= place_col, 1.0, 0.0), axis=1, keepdims=True)
    before = jnp.sum(jnp.where(start_row <= offset - 1, 1.0, 0.0), axis=1, keepdims=True)
    last = jnp.sum(jnp.where(start_row <= offset + T - 1, 1.0, 0.0), axis=1, keepdims=True)
    same = seg_col == seg_row
    allowed = jnp.logical_and(rows >= cols, same)
    allowed_t = jnp.logical_and(cols >= rows, same)
    living_col = jnp.where(seg_col == before, 1.0, 0.0)
    ending_col = jnp.where(seg_col == last, 1.0, 0.0)
    living_row = jnp.where(seg_row == before, 1.0, 0.0)
    ending_row = jnp.where(seg_row == last, 1.0, 0.0)
    through_flag = jnp.where(last == before, 1.0, 0.0)

    dt = dt_ref[...]
    cum_dt, dt_t, cum_row = jnp.zeros((T, H), f32), jnp.zeros((T, H), f32), jnp.zeros((H, T), f32)
    for piece in split(dt, 3):
        cum_dt = cum_dt + nt(tril, piece)
        dt_t = dt_t + nt(eye, piece)
        cum_row = cum_row + nt(piece, tril)
    rate = -jnp.exp(alog_ref[...])
    cum = cum_dt * rate
    alpha = jnp.exp(cum)
    beta = jnp.exp(-cum) * dt_t
    spread = jnp.concatenate(
        [
            jnp.concatenate(split(alpha, 3), axis=1),
            jnp.concatenate(split(beta, 3), axis=1),
        ],
        axis=0,
    )
    skip3 = jnp.concatenate(split(jnp.broadcast_to(skip_ref[...], (16, H)), 3), axis=1)

    bt, ct = bt_ref[...], ct_ref[...]
    b32, c32 = nt(eye, bt), nt(eye, ct)
    bb, cc = b32.astype(bf16), c32.astype(bf16)
    eb_t = (bt.astype(f32) * ending_row).astype(bf16)
    lc_t = (ct.astype(f32) * living_row).astype(bf16)
    eb_t = jnp.concatenate([eb_t, eb_t], axis=1)
    lc_t = jnp.concatenate([lc_t, lc_t], axis=1)
    eb = (b32 * ending_col).astype(bf16)
    lc = (c32 * living_col).astype(bf16)
    eb = jnp.concatenate([eb, eb], axis=1)
    lc = jnp.concatenate([lc, lc], axis=1)

    sent = []

    def send(src, dst, ssem, rsem, target):
        copy = pltpu.make_async_remote_copy(
            src_ref=src, dst_ref=dst, send_sem=ssem, recv_sem=rsem, device_id=target, device_id_type=MESH
        )
        copy.start()
        sent.append(copy)

    stored = []

    def store_out(src, dst):
        copy = pltpu.make_async_copy(src, dst, store.at[len(stored)])
        copy.start()
        stored.append(copy)

    def arrived(ref, sem):
        pltpu.make_async_remote_copy(
            src_ref=ref, dst_ref=ref, send_sem=sem, recv_sem=sem, device_id=(dp, me), device_id_type=MESH
        ).wait_recv()

    for k in range(CHUNKS):
        at = slice(k * C, (k + 1) * C)
        hot = one_hot(k, 3)
        wide = nn(spread, hot)
        alpha_w, beta_w = wide[:T], wide[T:]
        for copy in loads[small + 2 * k : small + 2 * k + 2]:
            copy.wait()
        g = g_ref[:, at].astype(f32)
        x = x_ref[:, at].astype(f32)
        g_hi, g_lo = split(g * alpha_w, 2)
        x_hi, x_lo = split(x * beta_w, 2)
        gh[0:T, at], gh[T : 2 * T, at] = g_hi, g_lo
        xh[0:T, at], xh[T : 2 * T, at] = x_hi, x_lo
        last_alpha = alpha_w[T - 1 : T]
        states = nn(eb_t, xh[:, at]) * last_alpha
        backs = nn(lc_t, gh[:, at])
        through = jnp.broadcast_to(last_alpha * through_flag, (8, C))
        for q in range(RING):
            part = slice(q * W, (q + 1) * W)
            sa[q, k, 0:N, :] = states[:, part]
            sa[q, k, N : 2 * N, :] = backs[:, part]
            sa[q, k, 2 * N : 2 * N + 8, :] = through[:, part]
        if k == 0:
            pl.semaphore_wait(barrier, len(greeted))
        for _, q in y_peers:
            send(sa.at[q, k], ra.at[y, k], sa_send.at[q, k], sa_recv.at[y, k], (dp, group * RING + q))
        ra[y, k] = sa[y, k]
        rowv[0:8, at] = nn(skip3, hot)[0:8]
        rowv[8:16, at] = jnp.broadcast_to(last_alpha, (8, C))
        vecs[:, at] = jnp.broadcast_to(jnp.sum(g * x, axis=0, keepdims=True), (8, C))
        bd[:, at] = beta_w

    s_hi, s_lo = split(jnp.where(allowed, nn(cc, bt), 0.0), 2)
    t_hi, t_lo = split(jnp.where(allowed_t, nn(bb, ct), 0.0), 2)
    s_hi = jnp.concatenate([s_hi, s_hi], axis=1)
    t_hi = jnp.concatenate([t_hi, t_hi], axis=1)
    both = jnp.zeros((T, 2 * T), f32)
    rest = jnp.zeros((T, T), f32)
    for k in range(CHUNKS):
        at = slice(k * C, (k + 1) * C)
        xp, gp = xh[:, at], gh[:, at]
        z2[:, at] = nn(s_hi, xp) + nn(s_lo, xp[:T])
        z1[:, at] = nn(t_hi, gp) + nn(t_lo, gp[:T])
        both = both + nt(gp[:T], xp)
        rest = rest + nt(gp[T:], xp[:T])
    ds = jnp.where(allowed, both[:, :T] + both[:, T:] + rest, 0.0)
    dc, db = jnp.zeros((N, T), f32), jnp.zeros((N, T), f32)
    for piece in split(ds, 2):
        dc = dc + nt(bt, piece)
        db = db + nn(ct, piece)

    def through_of(r, k):
        return ra[r, k, 2 * N : 2 * N + 1, :]

    def own(r, k):
        return ra[r, k, 0:N, :]

    def pulled(r, k):
        return ra[r, k, N : 2 * N, :]

    def total(k):
        for _, q in y_peers:
            arrived(ra.at[q, k], sa_recv.at[q, k])
        up, down = own(0, k), pulled(RING - 1, k)
        across = through_of(0, k)
        for i in range(1, RING):
            j = RING - 1 - i
            up = own(i, k) + through_of(i, k) * up
            down = pulled(j, k) + through_of(j, k) * down
            across = across * through_of(i, k)
        for side, value in ((0, up), (1, down)):
            s1[k, side, 0:N, :] = value
            s1[k, side, N : N + 8, :] = jnp.broadcast_to(across, (8, W))
            send(s1.at[k, side], r1.at[k, side], s1_send.at[k, side], r1_recv.at[k, side], z_near[side])

    def pair(k):
        for side in (0, 1):
            arrived(r1.at[k, side], r1_recv.at[k, side])
            across = s1[k, side, N : N + 8, :]
            s2[k, side, 0:N, :] = s1[k, side, 0:N, :] + across[0:1] * r1[k, side, 0:N, :]
            s2[k, side, N : N + 8, :] = across * r1[k, side, N : N + 8, :]
            send(
                s2.at[k, side, 0:N, :], r3.at[k, side], s3_send.at[k, side], r3_recv.at[k, side], z_far[side]
            )
            send(s2.at[k, side], r2.at[k, side], s2_send.at[k, side], r2_recv.at[k, side], z_near[side])

    def give(k):
        enters = []
        for side in (0, 1):
            arrived(r2.at[k, side], r2_recv.at[k, side])
            arrived(r3.at[k, side], r3_recv.at[k, side])
            enters.append(r2[k, side, 0:N, :] + r2[k, side, N : N + 1, :] * r3[k, side])
        up, down = enters
        for i in range(RING):
            j = RING - 1 - i
            sc[i, k, 0:N, :] = up
            sc[j, k, N : 2 * N, :] = down
            if i + 1 < RING:
                up = own(i, k) + through_of(i, k) * up
                down = pulled(j, k) + through_of(j, k) * down
        for _, q in y_peers:
            send(sc.at[q, k], rc.at[y, k], sc_send.at[q, k], sc_recv.at[y, k], (dp, group * RING + q))
        rc[y, k] = sc[y, k]

    sums = [jnp.zeros((H, 2 * T), f32), jnp.zeros((H, 2 * T), f32), jnp.zeros((2 * N, 2 * T), f32), jnp.zeros((2 * N, 2 * T), f32), jnp.zeros((H, 8), f32)]

    def finish(k):
        at = slice(k * C, (k + 1) * C)
        for _, q in y_peers:
            arrived(rc.at[q, k], sc_recv.at[q, k])
        hot = one_hot(k, 1)
        state = jnp.concatenate([rc[q, k, 0:N, :] for q in range(RING)], axis=1)
        later = jnp.concatenate([rc[q, k, N : 2 * N, :] for q in range(RING)], axis=1)
        mine = jnp.concatenate([sa[q, k, 0:N, :] for q in range(RING)], axis=1)
        last_alpha = rowv[8:9, at]
        leaving = jnp.sum(later * (mine + last_alpha * through_flag * state), axis=0, keepdims=True)
        first_row = lax.broadcasted_iota(jnp.int32, (8, C), 0) == 0
        vec = jnp.where(first_row, leaving, vecs[:, at])
        hh = jnp.concatenate(split(state, 2), axis=0)
        fh = jnp.concatenate(split(later * last_alpha, 2), axis=0)
        z1_w = z1[:, at] + nn(eb, fh)
        z2_w = z2[:, at] + nn(lc, hh)
        gp, xp = gh[:, at], xh[:, at]
        p1 = z1_w * (xp[:T].astype(f32) + xp[T:].astype(f32))
        p2 = z2_w * (gp[:T].astype(f32) + gp[T:].astype(f32))
        dx_ref[:, at] = (bd[:, at] * z1_w + rowv[0:1, at] * g_ref[:, at].astype(f32)).astype(bf16)
        store_out(dx_ref.at[:, at], dx_hbm.at[:, at])
        sums[0] = sums[0] + nt(hot, jnp.concatenate(split(p1, 2), axis=0))
        sums[1] = sums[1] + nt(hot, jnp.concatenate(split(p2, 2), axis=0))
        sums[2] = sums[2] + nt(hh, gp)
        sums[3] = sums[3] + nt(fh, xp)
        for piece in split(vec, 3):
            sums[4] = sums[4] + nt(hot, piece)

    steps = {"total": total, "pair": pair, "give": give, "finish": finish}
    for name, k in ORDER:
        steps[name](k)

    col_q = sums[0][:, :T] + sums[0][:, T:]
    row_q = sums[1][:, :T] + sums[1][:, T:]
    d_cum = row_q - col_q
    d_end, d_skip = sums[4][:, 0:1], sums[4][:, 1:2]
    rate_c = jnp.sum(jnp.where(head_r == head_c, jnp.broadcast_to(rate, (H, H)), 0.0), axis=1, keepdims=True)
    at_end = cols[:H] == T - 1
    d_alog = rate_c * jnp.sum((d_cum + jnp.where(at_end, d_end, 0.0)) * cum_row, axis=1, keepdims=True)
    diagonal = rows[:H] == cols[:H]
    alog_row = jnp.sum(jnp.where(diagonal, d_alog, 0.0), axis=0, keepdims=True)
    skip_row = jnp.sum(jnp.where(diagonal, d_skip, 0.0), axis=0, keepdims=True)
    row8 = lax.broadcasted_iota(jnp.int32, (8, T), 0)
    part = jnp.where(row8 == 0, alog_row, jnp.where(row8 == 1, skip_row, 0.0))

    stages = (
        (y, RING, [(dp, group * RING + (y + d) % RING) for d in range(1, RING)]),
        (z, n_z, z_peers),
        (fold, n_dp * n_x, f_peers),
    )
    for s, (mine, count, peers) in enumerate(stages):
        ar[s, mine] = part
        for d, target in enumerate(peers, 1):
            send(ar.at[s, mine], ar.at[s, mine], ar_send.at[s, d], ar_recv.at[s, mine], target)
        if s == 0:
            acc = sums[2][:N] + sums[2][N:]
            dc_ref[...] = (dc + living_row * (acc[:, :T] + acc[:, T:])).astype(bf16)
            acc = sums[3][:N] + sums[3][N:]
            db_ref[...] = (db + ending_row * (acc[:, :T] + acc[:, T:])).astype(bf16)
            d_log = jnp.zeros((H, T), f32) + d_end
            for piece in split(d_cum, 3):
                d_log = d_log + nn(piece, tril)
            dstep_ref[...] = col_q / dt + d_log * rate_c
            for src, dst in ((dc_ref, dc_hbm), (db_ref, db_hbm), (dstep_ref, dstep_hbm)):
                store_out(src, dst)
        for d in range(1, count):
            other = (mine + d) % count
            arrived(ar.at[s, other], ar_recv.at[s, other])
        part = ar[s, 0]
        for i in range(1, count):
            part = part + ar[s, i]
    dalog_ref[...] = part[0:1, :H]
    dskip_ref[...] = part[1:2, :H]
    store_out(dalog_ref, dalog_hbm)
    store_out(dskip_ref, dskip_hbm)
    for copy in sent:
        copy.wait_send()
    for copy in stored:
        copy.wait()


def write_out(count, *refs):
    sem = refs[-1]
    copies = [pltpu.make_async_copy(refs[i], refs[count + i], sem.at[i]) for i in range(count)]
    for copy in copies:
        copy.start()
    for copy in copies:
        copy.wait()


def per_device(n_dp, n_ctx, n_z, inputs, b_proj, c_proj, step_sizes, a_log, skip_gain, doc_lengths, grad_out):
    T, H, N = inputs.shape[1], a_log.shape[0], b_proj.shape[2]
    D, DOCS = inputs.shape[2] // H, doc_lengths.shape[1]
    HD = H * D
    K, W = CHUNKS, HD // (RING * CHUNKS)
    assert 4 * RING * T >= MOST_DOC
    n_x = n_ctx // (n_z * RING)
    slots = max(RING, n_z, n_dp * n_x)
    dims = (n_dp, n_ctx, n_z, T, H, D, N, DOCS)
    hbm = pl.BlockSpec(memory_space=pltpu.HBM)
    dma = pltpu.SemaphoreType.DMA
    outs = (
        jax.ShapeDtypeStruct((T, HD), bf16),
        jax.ShapeDtypeStruct((N, T), bf16),
        jax.ShapeDtypeStruct((N, T), bf16),
        jax.ShapeDtypeStruct((H, T), f32),
        jax.ShapeDtypeStruct((1, H), f32),
        jax.ShapeDtypeStruct((1, H), f32),
    )
    results = pl.pallas_call(
        functools.partial(kernel, dims),
        out_shape=outs,
        in_specs=[hbm] * 8,
        out_specs=(hbm,) * 6,
        scratch_shapes=[
            *(pltpu.VMEM(o.shape, o.dtype) for o in outs),
            pltpu.VMEM((T, HD), bf16),
            pltpu.VMEM((T, HD), bf16),
            pltpu.VMEM((N, T), bf16),
            pltpu.VMEM((N, T), bf16),
            pltpu.VMEM((H, T), f32),
            pltpu.VMEM((1, H), f32),
            pltpu.VMEM((1, H), f32),
            pltpu.VMEM((1, DOCS), jnp.int32),
            pltpu.VMEM((2 * T, HD), bf16),
            pltpu.VMEM((2 * T, HD), bf16),
            pltpu.VMEM((T, HD), f32),
            pltpu.VMEM((T, HD), f32),
            pltpu.VMEM((T, HD), f32),
            pltpu.VMEM((16, HD), f32),
            pltpu.VMEM((8, HD), f32),
            pltpu.VMEM((RING, K, 2 * N + 8, W), f32),
            pltpu.VMEM((RING, K, 2 * N + 8, W), f32),
            pltpu.VMEM((K, 2, N + 8, W), f32),
            pltpu.VMEM((K, 2, N + 8, W), f32),
            pltpu.VMEM((K, 2, N + 8, W), f32),
            pltpu.VMEM((K, 2, N + 8, W), f32),
            pltpu.VMEM((K, 2, N, W), f32),
            pltpu.VMEM((RING, K, 2 * N, W), f32),
            pltpu.VMEM((RING, K, 2 * N, W), f32),
            pltpu.VMEM((3, slots, 8, 128), f32),
            dma((6 + 2 * K,)),
            dma((5 + K,)),
            dma((RING, K)),
            dma((RING, K)),
            dma((K, 2)),
            dma((K, 2)),
            dma((K, 2)),
            dma((K, 2)),
            dma((K, 2)),
            dma((K, 2)),
            dma((RING, K)),
            dma((RING, K)),
            dma((3, slots)),
            dma((3, slots)),
        ],
        compiler_params=pltpu.CompilerParams(
            collective_id=0, has_side_effects=True, vmem_limit_bytes=60 << 20
        ),
        name="ssd_backward",
    )(
        inputs[0], grad_out[0], b_proj[0].T, c_proj[0].T, step_sizes[0],
        a_log[None], skip_gain[None], doc_lengths,
    )
    dx, db, dc, dstep, dalog, dskip = pl.pallas_call(
        functools.partial(write_out, len(outs)),
        out_shape=outs,
        in_specs=[hbm] * 6,
        out_specs=(hbm,) * 6,
        scratch_shapes=[dma((len(outs),))],
        name="write_out",
    )(*results)
    return dx[None], db.T[None], dc.T[None], dstep[None], dalog[0], dskip[0]


def solution(mesh):
    tokens, heads = P("dp", "ctx", None), P("dp", None, "ctx")
    n_dp, n_ctx = mesh.shape["dp"], mesh.shape["ctx"]
    n_z = min(8, n_ctx // RING)
    return jax.shard_map(
        functools.partial(per_device, n_dp, n_ctx, n_z),
        mesh=mesh,
        in_specs=(tokens, tokens, tokens, heads, P(), P(), P("dp", None), tokens),
        out_specs=(tokens, tokens, tokens, heads, P(), P()),
        check_vma=False,
    )
```

time: 75.5 us -> 76 us (level)
  Pallas kernels: 67 us -> 75.3 us
  local copies, waits for them, and re-layouts: 7.52 us -> 0 us
    pallas_call x1 -> x2, Pallas kernels: 67 us -> 75.3 us  [the longest x1 56.7 us: per_device(): pl.pallas_call(functools.partial(kernel, dims), out_shape=outs, in_specs=...]
    unnamed x22 -> x0, local copies, waits for them, and re-layouts: 7.52 us -> none
where the time goes in v2:
time: 76 us; the launch traced here: 75.9 us
  Pallas kernels  75.3 us (99%)
    pallas_call x1, Pallas kernels, per_device(): pl.pallas_call(functools.partial(kernel, dims), out_shape=outs, in_specs=...  56.7 us
    pallas_call x1, Pallas kernels, per_device(): pl.pallas_call(functools.partial(write_out, len(outs)), out_shape=outs, i...  18.6 us

profile of v2, /device:TPU:1, one launch (start us, length us, event | category | flops | bytes accessed | tf_op | source)
XLA Modules:
  0.0 75.9 jit_solution(13210698595490840572)
XLA Ops:
  0.6 56.7 %ssd_backward.1 = (bf16[128,2048]{1,0:T(8,128)(2,1)}, bf16[64,128]{1,0:T(8,128)(2,1)}, bf16[64,128]{1,0:T(8,128)(2,1)}, f32[32,128]{1,0:T(8,128)}, f32[1,32]{1,0:T(1,128)}, /*index=5*/f32[1,32]{1,0:T(1,128)}) custom-call(bf16[128,2048]{1,0:T(8,128)(2,1)} %bitcast.21, bf16[128,2048]{1,0:T(8,128)(2,1)} %bitcast.22, bf16[64,128]{1,0:T(8,128)(2,1)} %bitcast.23, ...), custom_call_target="tpu_custom_call" | custom-call | tf_op jit(solution)/shard_map/ssd_backward/pallas_call | solution.py:387
  57.3 18.6 %write_out.1 = (bf16[128,2048]{1,0:T(8,128)(2,1)}, bf16[64,128]{1,0:T(8,128)(2,1)}, bf16[64,128]{1,0:T(8,128)(2,1)}, f32[32,128]{1,0:T(8,128)}, f32[1,32]{1,0:T(1,128)}, /*index=5*/f32[1,32]{1,0:T(1,128)}) custom-call(bf16[128,2048]{1,0:T(8,128)(2,1)} %get-tuple-element.18.refs_0_, bf16[64,128]{1,0:T(8,128)(2,1)} %get-tuple-element.19.refs_1_, ...), custom_call_target="tpu_custom_call" | custom-call | tf_op jit(solution)/shard_map/write_out/pallas_call | solution.py:442

commit v3 on v2

--- a/solution.py
+++ b/solution.py
@@ -356,13 +356,19 @@
         copy.wait()
 
 
-def write_out(count, *refs):
-    sem = refs[-1]
-    copies = [pltpu.make_async_copy(refs[i], refs[count + i], sem.at[i]) for i in range(count)]
-    for copy in copies:
-        copy.start()
-    for copy in copies:
-        copy.wait()
+def write_out(plan, *refs):
+    count = len(refs) // 3
+    sources, targets, places, loaded, stored = refs[:count], refs[count : 2 * count], refs[2 * count : 3 * count], *refs[-2:]
+    copies = []
+    for n, (i, at) in enumerate(plan):
+        load = pltpu.make_async_copy(sources[i].at[:, at], places[i].at[:, at], loaded.at[n])
+        copies.append((load, pltpu.make_async_copy(places[i].at[:, at], targets[i].at[:, at], stored.at[n])))
+        load.start()
+    for load, store in copies:
+        load.wait()
+        store.start()
+    for _, store in copies:
+        store.wait()
 
 
 def per_device(n_dp, n_ctx, n_z, inputs, b_proj, c_proj, step_sizes, a_log, skip_gain, doc_lengths, grad_out):
@@ -439,12 +445,14 @@
         inputs[0], grad_out[0], b_proj[0].T, c_proj[0].T, step_sizes[0],
         a_log[None], skip_gain[None], doc_lengths,
     )
+    plan = [(0, slice(lo, lo + 512)) for lo in range(0, HD, 512)] + [(i, slice(None)) for i in range(1, len(outs))]
     dx, db, dc, dstep, dalog, dskip = pl.pallas_call(
-        functools.partial(write_out, len(outs)),
+        functools.partial(write_out, plan),
         out_shape=outs,
         in_specs=[hbm] * 6,
         out_specs=(hbm,) * 6,
-        scratch_shapes=[dma((len(outs),))],
+        scratch_shapes=[*(pltpu.VMEM(o.shape, o.dtype) for o in outs), dma((len(plan),)), dma((len(plan),))],
+        compiler_params=pltpu.CompilerParams(vmem_limit_bytes=60 << 20),
         name="write_out",
     )(*results)
     return dx[None], db.T[None], dc.T[None], dstep[None], dalog[0], dskip[0]

time: 76 us -> 59.4 us (0.78)
  Pallas kernels: 75.3 us -> 58.6 us
    pallas_call x1, Pallas kernels: 18.6 us -> 1.92 us  [per_device(): pl.pallas_call(functools.partial(write_out, plan), out_shape=outs, in_spe...]
where the time goes in v3:
time: 59.4 us; the launch traced here: 59.3 us
  Pallas kernels  58.6 us (99%)
  between operations  0.64 us (1%)
    pallas_call x1, Pallas kernels, per_device(): pl.pallas_call(functools.partial(kernel, dims), out_shape=outs, in_specs=...  56.7 us
    pallas_call x1, Pallas kernels, per_device(): pl.pallas_call(functools.partial(write_out, plan), out_shape=outs, in_spe...  1.92 us

profile of v3, /device:TPU:1, one launch (start us, length us, event | category | flops | bytes accessed | tf_op | source)
XLA Modules:
  0.0 59.3 jit_solution(9124400299810997885)
XLA Ops:
  0.6 56.7 %ssd_backward.1 = (bf16[128,2048]{1,0:T(8,128)(2,1)}, bf16[64,128]{1,0:T(8,128)(2,1)}, bf16[64,128]{1,0:T(8,128)(2,1)}, f32[32,128]{1,0:T(8,128)}, f32[1,32]{1,0:T(1,128)}, /*index=5*/f32[1,32]{1,0:T(1,128)}) custom-call(bf16[128,2048]{1,0:T(8,128)(2,1)} %bitcast.21, bf16[128,2048]{1,0:T(8,128)(2,1)} %bitcast.22, bf16[64,128]{1,0:T(8,128)(2,1)} %bitcast.23, ...), custom_call_target="tpu_custom_call" | custom-call | tf_op jit(solution)/shard_map/ssd_backward/pallas_call | solution.py:393
  57.3 1.9 %write_out.1 = (bf16[128,2048]{1,0:T(8,128)(2,1)}, bf16[64,128]{1,0:T(8,128)(2,1)}, bf16[64,128]{1,0:T(8,128)(2,1)}, f32[32,128]{1,0:T(8,128)}, f32[1,32]{1,0:T(1,128)}, /*index=5*/f32[1,32]{1,0:T(1,128)}) custom-call(bf16[128,2048]{1,0:T(8,128)(2,1)} %get-tuple-element.18.refs_0_, bf16[64,128]{1,0:T(8,128)(2,1)} %get-tuple-element.19.refs_1_, ...), custom_call_target="tpu_custom_call" | custom-call | tf_op jit(solution)/shard_map/write_out/pallas_call | solution.py:449

commit v4 on v3

--- a/solution.py
+++ b/solution.py
@@ -44,7 +44,7 @@
     dx_ref, db_ref, dc_ref, dstep_ref, dalog_ref, dskip_ref,
     x_ref, g_ref, bt_ref, ct_ref, dt_ref, alog_ref, skip_ref, len_ref,
     xh, gh, bd, z1, z2, rowv, vecs, sa, ra, s1, r1, s2, r2, r3, sc, rc, ar,
-    load, store, sa_send, sa_recv, s1_send, r1_recv, s2_send, r2_recv, s3_send, r3_recv, sc_send, sc_recv, ar_send, ar_recv,
+    load, store, sa_send, sa_recv, s1_send, r1_recv, s2_send, r2_recv, s3_send, r3_recv, sc_send, sc_recv, ar_send, ar_recv, known,
 ):
     n_dp, n_ctx, n_z, T, H, D, N, DOCS = dims
     n_x = n_ctx // (n_z * RING)
@@ -58,18 +58,18 @@
     y_peers = [(d, (y + d) % RING) for d in (2, 1, 3)]
     z_near = [(dp, ((group + d) % groups) * RING + y) for d in (1, groups - 1)]
     z_far = [(dp, ((group + d + groups) % groups) * RING + y) for d in (3, -3)]
-    z_peers = [(dp, (xhi * n_z + (z + d) % n_z) * RING + y) for d in range(1, n_z)]
-    fold = dp * n_x + xhi
-    f_peers = []
-    for d in range(1, n_dp * n_x):
-        other = (fold + d) % (n_dp * n_x)
-        f_peers.append((other // n_x, ((other % n_x) * n_z + z) * RING + y))
-
-    barrier = pltpu.get_barrier_semaphore()
-    greeted = [(dp, group * RING + q) for _, q in y_peers]
-    greeted += z_near + z_far + z_peers + f_peers
-    for target in greeted:
-        pl.semaphore_signal(barrier, inc=1, device_id=target, device_id_type=MESH)
+    n_core = 2 - n_dp % 2
+    xlo, core = dp // n_core, dp % n_core
+    n_plane, n_line = RING * (n_dp // n_core) * n_x, n_z * n_core
+    plane, line = (xlo * n_x + xhi) * RING + y, z * n_core + core
+    plane_peers, line_peers = [], []
+    for d in range(1, n_plane):
+        other = (plane + d) % n_plane
+        across = other // RING
+        plane_peers.append(((across // n_x) * n_core + core, ((across % n_x) * n_z + z) * RING + other % RING))
+    for d in range(1, n_line):
+        other = (line + d) % n_line
+        line_peers.append((xlo * n_core + other % n_core, (xhi * n_z + other // n_core) * RING + y))
 
     pairs = [(len_hbm, len_ref), (dt_hbm, dt_ref), (alog_hbm, alog_ref), (bt_hbm, bt_ref), (ct_hbm, ct_ref), (skip_hbm, skip_ref)]
     small = len(pairs)
@@ -77,7 +77,22 @@
         at = slice(k * C, (k + 1) * C)
         pairs += [(g_hbm.at[:, at], g_ref.at[:, at]), (x_hbm.at[:, at], x_ref.at[:, at])]
     loads = [pltpu.make_async_copy(a, b, load.at[i]) for i, (a, b) in enumerate(pairs)]
-    for copy in loads:
+    for copy in loads[: small + 2]:
+        copy.start()
+
+    x_peers, core_peers = [], []
+    for d in range(1, n_plane // RING):
+        other = (plane // RING + d) % (n_plane // RING)
+        x_peers.append(((other // n_x) * n_core + core, ((other % n_x) * n_z + z) * RING + y))
+    for d in range(1, n_core):
+        core_peers.append((xlo * n_core + (core + d) % n_core, me))
+    barrier = pltpu.get_barrier_semaphore()
+    greeted = [(dp, group * RING + q) for _, q in y_peers]
+    greeted += z_near + z_far + x_peers + core_peers
+    greeted += [(dp, (xhi * n_z + (z + d) % n_z) * RING + y) for d in range(1, n_z)]
+    for target in greeted:
+        pl.semaphore_signal(barrier, inc=1, device_id=target, device_id_type=MESH)
+    for copy in loads[small + 2 :]:
         copy.start()
 
     rows = lax.broadcasted_iota(jnp.int32, (T, T), 0)
@@ -169,7 +184,13 @@
             src_ref=ref, dst_ref=ref, send_sem=sem, recv_sem=sem, device_id=(dp, me), device_id_type=MESH
         ).wait_recv()
 
-    for k in range(CHUNKS):
+    s_hi, s_lo = split(jnp.where(allowed, nn(cc, bt), 0.0), 2)
+    t_hi, t_lo = split(jnp.where(allowed_t, nn(bb, ct), 0.0), 2)
+    s_hi = jnp.concatenate([s_hi, s_hi], axis=1)
+    t_hi = jnp.concatenate([t_hi, t_hi], axis=1)
+    scores = [jnp.zeros((T, 2 * T), f32), jnp.zeros((T, T), f32)]
+
+    def states(k):
         at = slice(k * C, (k + 1) * C)
         hot = one_hot(k, 3)
         wide = nn(spread, hot)
@@ -183,12 +204,12 @@
         gh[0:T, at], gh[T : 2 * T, at] = g_hi, g_lo
         xh[0:T, at], xh[T : 2 * T, at] = x_hi, x_lo
         last_alpha = alpha_w[T - 1 : T]
-        states = nn(eb_t, xh[:, at]) * last_alpha
+        own_states = nn(eb_t, xh[:, at]) * last_alpha
         backs = nn(lc_t, gh[:, at])
         through = jnp.broadcast_to(last_alpha * through_flag, (8, C))
         for q in range(RING):
             part = slice(q * W, (q + 1) * W)
-            sa[q, k, 0:N, :] = states[:, part]
+            sa[q, k, 0:N, :] = own_states[:, part]
             sa[q, k, N : 2 * N, :] = backs[:, part]
             sa[q, k, 2 * N : 2 * N + 8, :] = through[:, part]
         if k == 0:
@@ -201,20 +222,21 @@
         vecs[:, at] = jnp.broadcast_to(jnp.sum(g * x, axis=0, keepdims=True), (8, C))
         bd[:, at] = beta_w
 
-    s_hi, s_lo = split(jnp.where(allowed, nn(cc, bt), 0.0), 2)
-    t_hi, t_lo = split(jnp.where(allowed_t, nn(bb, ct), 0.0), 2)
-    s_hi = jnp.concatenate([s_hi, s_hi], axis=1)
-    t_hi = jnp.concatenate([t_hi, t_hi], axis=1)
-    both = jnp.zeros((T, 2 * T), f32)
-    rest = jnp.zeros((T, T), f32)
-    for k in range(CHUNKS):
+    def within(k):
         at = slice(k * C, (k + 1) * C)
         xp, gp = xh[:, at], gh[:, at]
         z2[:, at] = nn(s_hi, xp) + nn(s_lo, xp[:T])
         z1[:, at] = nn(t_hi, gp) + nn(t_lo, gp[:T])
-        both = both + nt(gp[:T], xp)
-        rest = rest + nt(gp[T:], xp[:T])
-    ds = jnp.where(allowed, both[:, :T] + both[:, T:] + rest, 0.0)
+        scores[0] = scores[0] + nt(gp[:T], xp)
+        scores[1] = scores[1] + nt(gp[T:], xp[:T])
+
+    for k in range(CHUNKS):
+        states(k)
+    for target in x_peers + core_peers:
+        pl.semaphore_signal(known, inc=1, device_id=target, device_id_type=MESH)
+    for k in range(CHUNKS):
+        within(k)
+    ds = jnp.where(allowed, scores[0][:, :T] + scores[0][:, T:] + scores[1], 0.0)
     dc, db = jnp.zeros((N, T), f32), jnp.zeros((N, T), f32)
     for piece in split(ds, 2):
         dc = dc + nt(bt, piece)
@@ -314,17 +336,11 @@
     rate_c = jnp.sum(jnp.where(head_r == head_c, jnp.broadcast_to(rate, (H, H)), 0.0), axis=1, keepdims=True)
     at_end = cols[:H] == T - 1
     d_alog = rate_c * jnp.sum((d_cum + jnp.where(at_end, d_end, 0.0)) * cum_row, axis=1, keepdims=True)
-    diagonal = rows[:H] == cols[:H]
-    alog_row = jnp.sum(jnp.where(diagonal, d_alog, 0.0), axis=0, keepdims=True)
-    skip_row = jnp.sum(jnp.where(diagonal, d_skip, 0.0), axis=0, keepdims=True)
-    row8 = lax.broadcasted_iota(jnp.int32, (8, T), 0)
-    part = jnp.where(row8 == 0, alog_row, jnp.where(row8 == 1, skip_row, 0.0))
-
-    stages = (
-        (y, RING, [(dp, group * RING + (y + d) % RING) for d in range(1, RING)]),
-        (z, n_z, z_peers),
-        (fold, n_dp * n_x, f_peers),
-    )
+    part = jnp.where(rows[:H] == cols[:H], d_alog, jnp.where(rows[:H] + H == cols[:H], d_skip, 0.0))
+    part = jnp.sum(part, axis=0, keepdims=True)
+
+    stages = ((plane, n_plane, plane_peers), (line, n_line, line_peers))
+    pl.semaphore_wait(known, len(x_peers) + len(core_peers))
     for s, (mine, count, peers) in enumerate(stages):
         ar[s, mine] = part
         for d, target in enumerate(peers, 1):
@@ -346,8 +362,8 @@
         part = ar[s, 0]
         for i in range(1, count):
             part = part + ar[s, i]
-    dalog_ref[...] = part[0:1, :H]
-    dskip_ref[...] = part[1:2, :H]
+    dalog_ref[...] = part[:, :H]
+    dskip_ref[...] = part[:, H : 2 * H]
     store_out(dalog_ref, dalog_hbm)
     store_out(dskip_ref, dskip_hbm)
     for copy in sent:
@@ -378,7 +394,7 @@
     K, W = CHUNKS, HD // (RING * CHUNKS)
     assert 4 * RING * T >= MOST_DOC
     n_x = n_ctx // (n_z * RING)
-    slots = max(RING, n_z, n_dp * n_x)
+    slots = max(RING * n_dp * n_x, 2 * n_z)
     dims = (n_dp, n_ctx, n_z, T, H, D, N, DOCS)
     hbm = pl.BlockSpec(memory_space=pltpu.HBM)
     dma = pltpu.SemaphoreType.DMA
@@ -421,7 +437,7 @@
             pltpu.VMEM((K, 2, N, W), f32),
             pltpu.VMEM((RING, K, 2 * N, W), f32),
             pltpu.VMEM((RING, K, 2 * N, W), f32),
-            pltpu.VMEM((3, slots, 8, 128), f32),
+            pltpu.VMEM((2, slots, 1, 128), f32),
             dma((6 + 2 * K,)),
             dma((5 + K,)),
             dma((RING, K)),
@@ -434,8 +450,9 @@
             dma((K, 2)),
             dma((RING, K)),
             dma((RING, K)),
-            dma((3, slots)),
-            dma((3, slots)),
+            dma((2, slots)),
+            dma((2, slots)),
+            pltpu.SemaphoreType.REGULAR,
         ],
         compiler_params=pltpu.CompilerParams(
             collective_id=0, has_side_effects=True, vmem_limit_bytes=60 << 20

time: 59.4 us -> 58.2 us (0.980)
  Pallas kernels: 58.6 us -> 57.4 us
    pallas_call x1, Pallas kernels: 56.7 us -> 55.4 us  [per_device(): pl.pallas_call(functools.partial(kernel, dims), out_shape=outs, in_specs=...]
where the time goes in v4:
time: 58.2 us; the launch traced here: 58 us
  Pallas kernels  57.4 us (99%)
  between operations  0.64 us (1%)
    pallas_call x1, Pallas kernels, per_device(): pl.pallas_call(functools.partial(kernel, dims), out_shape=outs, in_specs=...  55.4 us
    pallas_call x1, Pallas kernels, per_device(): pl.pallas_call(functools.partial(write_out, plan), out_shape=outs, in_spe...  1.92 us

profile of v4, /device:TPU:1, one launch (start us, length us, event | category | flops | bytes accessed | tf_op | source)
XLA Modules:
  0.0 58.0 jit_solution(4915414560697141065)
XLA Ops:
  0.6 55.4 %ssd_backward.1 = (bf16[128,2048]{1,0:T(8,128)(2,1)}, bf16[64,128]{1,0:T(8,128)(2,1)}, bf16[64,128]{1,0:T(8,128)(2,1)}, f32[32,128]{1,0:T(8,128)}, f32[1,32]{1,0:T(1,128)}, /*index=5*/f32[1,32]{1,0:T(1,128)}) custom-call(bf16[128,2048]{1,0:T(8,128)(2,1)} %bitcast.21, bf16[128,2048]{1,0:T(8,128)(2,1)} %bitcast.22, bf16[64,128]{1,0:T(8,128)(2,1)} %bitcast.23, ...), custom_call_target="tpu_custom_call" | custom-call | tf_op jit(solution)/shard_map/ssd_backward/pallas_call | solution.py:409
  56.1 1.9 %write_out.1 = (bf16[128,2048]{1,0:T(8,128)(2,1)}, bf16[64,128]{1,0:T(8,128)(2,1)}, bf16[64,128]{1,0:T(8,128)(2,1)}, f32[32,128]{1,0:T(8,128)}, f32[1,32]{1,0:T(1,128)}, /*index=5*/f32[1,32]{1,0:T(1,128)}) custom-call(bf16[128,2048]{1,0:T(8,128)(2,1)} %get-tuple-element.18.refs_0_, bf16[64,128]{1,0:T(8,128)(2,1)} %get-tuple-element.19.refs_1_, ...), custom_call_target="tpu_custom_call" | custom-call | tf_op jit(solution)/shard_map/write_out/pallas_call | solution.py:466

commit v5 on v4

--- a/solution.py
+++ b/solution.py
@@ -43,8 +43,8 @@
     dx_hbm, db_hbm, dc_hbm, dstep_hbm, dalog_hbm, dskip_hbm,
     dx_ref, db_ref, dc_ref, dstep_ref, dalog_ref, dskip_ref,
     x_ref, g_ref, bt_ref, ct_ref, dt_ref, alog_ref, skip_ref, len_ref,
-    xh, gh, bd, z1, z2, rowv, vecs, sa, ra, s1, r1, s2, r2, r3, sc, rc, ar,
-    load, store, sa_send, sa_recv, s1_send, r1_recv, s2_send, r2_recv, s3_send, r3_recv, sc_send, sc_recv, ar_send, ar_recv, known,
+    xh, gh, bd, z1, z2, rowv, vecs, sa, ra, st, rt, s1, r1, s2, r2, r3, sc, rc, ar,
+    load, store, sa_send, sa_recv, s1_send, r1_recv, s2_send, r2_recv, s3_send, r3_recv, sc_send, sc_recv, st_send, rt_recv, ar_send, ar_recv, known,
 ):
     n_dp, n_ctx, n_z, T, H, D, N, DOCS = dims
     n_x = n_ctx // (n_z * RING)
@@ -61,15 +61,21 @@
     n_core = 2 - n_dp % 2
     xlo, core = dp // n_core, dp % n_core
     n_plane, n_line = RING * (n_dp // n_core) * n_x, n_z * n_core
-    plane, line = (xlo * n_x + xhi) * RING + y, z * n_core + core
     plane_peers, line_peers = [], []
-    for d in range(1, n_plane):
-        other = (plane + d) % n_plane
-        across = other // RING
-        plane_peers.append(((across // n_x) * n_core + core, ((across % n_x) * n_z + z) * RING + other % RING))
-    for d in range(1, n_line):
-        other = (line + d) % n_line
-        line_peers.append((xlo * n_core + other % n_core, (xhi * n_z + other // n_core) * RING + y))
+    n_lane = n_plane // RING
+    lane, n_xlo = xhi * (n_dp // n_core) + xlo, n_dp // n_core
+    plane, line = lane * RING + y, z * n_core + core
+
+    def far(step, size):
+        return min(step, size - step)
+
+    steps = [(a, b) for a in range(n_lane) for b in range(RING) if (a, b) != (0, 0)]
+    for a, b in sorted(steps, key=lambda s: -far(s[0], n_lane) - far(s[1], RING)):
+        other = (lane + a) % n_lane
+        plane_peers.append(((other % n_xlo) * n_core + core, ((other // n_xlo) * n_z + z) * RING + (y + b) % RING))
+    steps = [(a, b) for a in range(n_z) for b in range(n_core) if (a, b) != (0, 0)]
+    for a, b in sorted(steps, key=lambda s: -far(s[0], n_z) - 0.5 * s[1]):
+        line_peers.append((xlo * n_core + (core + b) % n_core, (xhi * n_z + (z + a) % n_z) * RING + y))
 
     pairs = [(len_hbm, len_ref), (dt_hbm, dt_ref), (alog_hbm, alog_ref), (bt_hbm, bt_ref), (ct_hbm, ct_ref), (skip_hbm, skip_ref)]
     small = len(pairs)
@@ -81,11 +87,11 @@
         copy.start()
 
     x_peers, core_peers = [], []
-    for d in range(1, n_plane // RING):
-        other = (plane // RING + d) % (n_plane // RING)
-        x_peers.append(((other // n_x) * n_core + core, ((other % n_x) * n_z + z) * RING + y))
-    for d in range(1, n_core):
-        core_peers.append((xlo * n_core + (core + d) % n_core, me))
+    for a in range(1, n_lane):
+        other = (lane + a) % n_lane
+        x_peers.append(((other % n_xlo) * n_core + core, ((other // n_xlo) * n_z + z) * RING + y))
+    for b in range(1, n_core):
+        core_peers.append((xlo * n_core + (core + b) % n_core, me))
     barrier = pltpu.get_barrier_semaphore()
     greeted = [(dp, group * RING + q) for _, q in y_peers]
     greeted += z_near + z_far + x_peers + core_peers
@@ -133,11 +139,10 @@
     through_flag = jnp.where(last == before, 1.0, 0.0)
 
     dt = dt_ref[...]
-    cum_dt, dt_t, cum_row = jnp.zeros((T, H), f32), jnp.zeros((T, H), f32), jnp.zeros((H, T), f32)
+    cum_dt, dt_t = jnp.zeros((T, H), f32), jnp.zeros((T, H), f32)
     for piece in split(dt, 3):
         cum_dt = cum_dt + nt(tril, piece)
         dt_t = dt_t + nt(eye, piece)
-        cum_row = cum_row + nt(piece, tril)
     rate = -jnp.exp(alog_ref[...])
     cum = cum_dt * rate
     alpha = jnp.exp(cum)
@@ -152,25 +157,22 @@
     skip3 = jnp.concatenate(split(jnp.broadcast_to(skip_ref[...], (16, H)), 3), axis=1)
 
     bt, ct = bt_ref[...], ct_ref[...]
-    b32, c32 = nt(eye, bt), nt(eye, ct)
-    bb, cc = b32.astype(bf16), c32.astype(bf16)
     eb_t = (bt.astype(f32) * ending_row).astype(bf16)
     lc_t = (ct.astype(f32) * living_row).astype(bf16)
     eb_t = jnp.concatenate([eb_t, eb_t], axis=1)
     lc_t = jnp.concatenate([lc_t, lc_t], axis=1)
-    eb = (b32 * ending_col).astype(bf16)
-    lc = (c32 * living_col).astype(bf16)
-    eb = jnp.concatenate([eb, eb], axis=1)
-    lc = jnp.concatenate([lc, lc], axis=1)
 
     sent = []
 
     def send(src, dst, ssem, rsem, target):
-        copy = pltpu.make_async_remote_copy(
+        pltpu.make_async_remote_copy(
             src_ref=src, dst_ref=dst, send_sem=ssem, recv_sem=rsem, device_id=target, device_id_type=MESH
+        ).start()
+
+    def waiter(ref, sem):
+        return pltpu.make_async_remote_copy(
+            src_ref=ref, dst_ref=ref, send_sem=sem, recv_sem=sem, device_id=(dp, me), device_id_type=MESH
         )
-        copy.start()
-        sent.append(copy)
 
     stored = []
 
@@ -179,16 +181,19 @@
         copy.start()
         stored.append(copy)
 
-    def arrived(ref, sem):
-        pltpu.make_async_remote_copy(
-            src_ref=ref, dst_ref=ref, send_sem=sem, recv_sem=sem, device_id=(dp, me), device_id_type=MESH
-        ).wait_recv()
-
-    s_hi, s_lo = split(jnp.where(allowed, nn(cc, bt), 0.0), 2)
-    t_hi, t_lo = split(jnp.where(allowed_t, nn(bb, ct), 0.0), 2)
-    s_hi = jnp.concatenate([s_hi, s_hi], axis=1)
-    t_hi = jnp.concatenate([t_hi, t_hi], axis=1)
-    scores = [jnp.zeros((T, 2 * T), f32), jnp.zeros((T, T), f32)]
+
+    per = C // D
+    row_k = lax.broadcasted_iota(jnp.int32, (8, H), 0)
+    head_l = lax.broadcasted_iota(jnp.int32, (8, H), 1)
+    mine = jnp.where(head_l // per == row_k, alpha[T - 1 : T] * through_flag, 0.0)
+    head_s = lax.broadcasted_iota(jnp.int32, (H, C), 0)
+    lane_s = lax.broadcasted_iota(jnp.int32, (H, C), 1)
+    spots = jnp.where(head_s % per == lane_s // D, 1.0, 0.0).astype(bf16)
+    tile = jnp.zeros((8, C), f32)
+    for piece in split(mine, 3):
+        tile = tile + nn(piece, spots)
+    for q in range(RING):
+        st[q] = tile[:, q * W : (q + 1) * W]
 
     def states(k):
         at = slice(k * C, (k + 1) * C)
@@ -206,16 +211,19 @@
         last_alpha = alpha_w[T - 1 : T]
         own_states = nn(eb_t, xh[:, at]) * last_alpha
         backs = nn(lc_t, gh[:, at])
-        through = jnp.broadcast_to(last_alpha * through_flag, (8, C))
         for q in range(RING):
             part = slice(q * W, (q + 1) * W)
             sa[q, k, 0:N, :] = own_states[:, part]
             sa[q, k, N : 2 * N, :] = backs[:, part]
-            sa[q, k, 2 * N : 2 * N + 8, :] = through[:, part]
         if k == 0:
             pl.semaphore_wait(barrier, len(greeted))
+            for _, q in y_peers:
+                send(st.at[q], rt.at[y], st_send.at[0], rt_recv.at[0], (dp, group * RING + q))
+            sent.append((st.at[0 : RING - 1], st_send.at[0]))
+            rt[y] = st[y]
         for _, q in y_peers:
-            send(sa.at[q, k], ra.at[y, k], sa_send.at[q, k], sa_recv.at[y, k], (dp, group * RING + q))
+            send(sa.at[q, k], ra.at[y, k], sa_send.at[k], sa_recv.at[k], (dp, group * RING + q))
+        sent.append((sa.at[0 : RING - 1, k], sa_send.at[k]))
         ra[y, k] = sa[y, k]
         rowv[0:8, at] = nn(skip3, hot)[0:8]
         rowv[8:16, at] = jnp.broadcast_to(last_alpha, (8, C))
@@ -234,6 +242,20 @@
         states(k)
     for target in x_peers + core_peers:
         pl.semaphore_signal(known, inc=1, device_id=target, device_id_type=MESH)
+    cum_row = jnp.zeros((H, T), f32)
+    for piece in split(dt, 3):
+        cum_row = cum_row + nt(piece, tril)
+    b32, c32 = nt(eye, bt), nt(eye, ct)
+    bb, cc = b32.astype(bf16), c32.astype(bf16)
+    eb = (b32 * ending_col).astype(bf16)
+    lc = (c32 * living_col).astype(bf16)
+    eb = jnp.concatenate([eb, eb], axis=1)
+    lc = jnp.concatenate([lc, lc], axis=1)
+    s_hi, s_lo = split(jnp.where(allowed, nn(cc, bt), 0.0), 2)
+    t_hi, t_lo = split(jnp.where(allowed_t, nn(bb, ct), 0.0), 2)
+    s_hi = jnp.concatenate([s_hi, s_hi], axis=1)
+    t_hi = jnp.concatenate([t_hi, t_hi], axis=1)
+    scores = [jnp.zeros((T, 2 * T), f32), jnp.zeros((T, T), f32)]
     for k in range(CHUNKS):
         within(k)
     ds = jnp.where(allowed, scores[0][:, :T] + scores[0][:, T:] + scores[1], 0.0)
@@ -243,7 +265,7 @@
         db = db + nn(ct, piece)
 
     def through_of(r, k):
-        return ra[r, k, 2 * N : 2 * N + 1, :]
+        return rt[r, k : k + 1, :]
 
     def own(r, k):
         return ra[r, k, 0:N, :]
@@ -252,8 +274,9 @@
         return ra[r, k, N : 2 * N, :]
 
     def total(k):
-        for _, q in y_peers:
-            arrived(ra.at[q, k], sa_recv.at[q, k])
+        if k == 0:
+            waiter(rt.at[0 : RING - 1], rt_recv.at[0]).wait_recv()
+        waiter(ra.at[0 : RING - 1, k], sa_recv.at[k]).wait_recv()
         up, down = own(0, k), pulled(RING - 1, k)
         across = through_of(0, k)
         for i in range(1, RING):
@@ -264,24 +287,25 @@
         for side, value in ((0, up), (1, down)):
             s1[k, side, 0:N, :] = value
             s1[k, side, N : N + 8, :] = jnp.broadcast_to(across, (8, W))
-            send(s1.at[k, side], r1.at[k, side], s1_send.at[k, side], r1_recv.at[k, side], z_near[side])
+            send(s1.at[k, side], r1.at[k, side], s1_send.at[k], r1_recv.at[k], z_near[side])
+        sent.append((s1.at[k], s1_send.at[k]))
 
     def pair(k):
+        waiter(r1.at[k], r1_recv.at[k]).wait_recv()
         for side in (0, 1):
-            arrived(r1.at[k, side], r1_recv.at[k, side])
             across = s1[k, side, N : N + 8, :]
             s2[k, side, 0:N, :] = s1[k, side, 0:N, :] + across[0:1] * r1[k, side, 0:N, :]
             s2[k, side, N : N + 8, :] = across * r1[k, side, N : N + 8, :]
-            send(
-                s2.at[k, side, 0:N, :], r3.at[k, side], s3_send.at[k, side], r3_recv.at[k, side], z_far[side]
-            )
-            send(s2.at[k, side], r2.at[k, side], s2_send.at[k, side], r2_recv.at[k, side], z_near[side])
+            send(s2.at[k, side, 0:N, :], r3.at[k, side], s3_send.at[k], r3_recv.at[k], z_far[side])
+            send(s2.at[k, side], r2.at[k, side], s2_send.at[k], r2_recv.at[k], z_near[side])
+        sent.append((r3.at[k], s3_send.at[k]))
+        sent.append((s2.at[k], s2_send.at[k]))
 
     def give(k):
         enters = []
+        waiter(r2.at[k], r2_recv.at[k]).wait_recv()
+        waiter(r3.at[k], r3_recv.at[k]).wait_recv()
         for side in (0, 1):
-            arrived(r2.at[k, side], r2_recv.at[k, side])
-            arrived(r3.at[k, side], r3_recv.at[k, side])
             enters.append(r2[k, side, 0:N, :] + r2[k, side, N : N + 1, :] * r3[k, side])
         up, down = enters
         for i in range(RING):
@@ -292,15 +316,15 @@
                 up = own(i, k) + through_of(i, k) * up
                 down = pulled(j, k) + through_of(j, k) * down
         for _, q in y_peers:
-            send(sc.at[q, k], rc.at[y, k], sc_send.at[q, k], sc_recv.at[y, k], (dp, group * RING + q))
+            send(sc.at[q, k], rc.at[y, k], sc_send.at[k], sc_recv.at[k], (dp, group * RING + q))
+        sent.append((sc.at[0 : RING - 1, k], sc_send.at[k]))
         rc[y, k] = sc[y, k]
 
     sums = [jnp.zeros((H, 2 * T), f32), jnp.zeros((H, 2 * T), f32), jnp.zeros((2 * N, 2 * T), f32), jnp.zeros((2 * N, 2 * T), f32), jnp.zeros((H, 8), f32)]
 
     def finish(k):
         at = slice(k * C, (k + 1) * C)
-        for _, q in y_peers:
-            arrived(rc.at[q, k], sc_recv.at[q, k])
+        waiter(rc.at[0 : RING - 1, k], sc_recv.at[k]).wait_recv()
         hot = one_hot(k, 1)
         state = jnp.concatenate([rc[q, k, 0:N, :] for q in range(RING)], axis=1)
         later = jnp.concatenate([rc[q, k, N : 2 * N, :] for q in range(RING)], axis=1)
@@ -316,15 +340,23 @@
         gp, xp = gh[:, at], xh[:, at]
         p1 = z1_w * (xp[:T].astype(f32) + xp[T:].astype(f32))
         p2 = z2_w * (gp[:T].astype(f32) + gp[T:].astype(f32))
-        dx_ref[:, at] = (bd[:, at] * z1_w + rowv[0:1, at] * g_ref[:, at].astype(f32)).astype(bf16)
-        store_out(dx_ref.at[:, at], dx_hbm.at[:, at])
         sums[0] = sums[0] + nt(hot, jnp.concatenate(split(p1, 2), axis=0))
         sums[1] = sums[1] + nt(hot, jnp.concatenate(split(p2, 2), axis=0))
-        sums[2] = sums[2] + nt(hh, gp)
-        sums[3] = sums[3] + nt(fh, xp)
         for piece in split(vec, 3):
             sums[4] = sums[4] + nt(hot, piece)
 
+        def remainder():
+            dx_ref[:, at] = (bd[:, at] * z1_w + rowv[0:1, at] * g_ref[:, at].astype(f32)).astype(bf16)
+            store_out(dx_ref.at[:, at], dx_hbm.at[:, at])
+            sums[2] = sums[2] + nt(hh, gp)
+            sums[3] = sums[3] + nt(fh, xp)
+
+        if k + 1 < CHUNKS:
+            remainder()
+        else:
+            put_off.append(remainder)
+
+    put_off = []
     steps = {"total": total, "pair": pair, "give": give, "finish": finish}
     for name, k in ORDER:
         steps[name](k)
@@ -343,9 +375,11 @@
     pl.semaphore_wait(known, len(x_peers) + len(core_peers))
     for s, (mine, count, peers) in enumerate(stages):
         ar[s, mine] = part
-        for d, target in enumerate(peers, 1):
-            send(ar.at[s, mine], ar.at[s, mine], ar_send.at[s, d], ar_recv.at[s, mine], target)
+        for target in peers:
+            send(ar.at[s, mine], ar.at[s, mine], ar_send.at[s], ar_recv.at[s], target)
         if s == 0:
+            for work in put_off:
+                work()
             acc = sums[2][:N] + sums[2][N:]
             dc_ref[...] = (dc + living_row * (acc[:, :T] + acc[:, T:])).astype(bf16)
             acc = sums[3][:N] + sums[3][N:]
@@ -356,9 +390,10 @@
             dstep_ref[...] = col_q / dt + d_log * rate_c
             for src, dst in ((dc_ref, dc_hbm), (db_ref, db_hbm), (dstep_ref, dstep_hbm)):
                 store_out(src, dst)
-        for d in range(1, count):
-            other = (mine + d) % count
-            arrived(ar.at[s, other], ar_recv.at[s, other])
+            for ref, sem in sent:
+                waiter(ref, sem).wait_send()
+        if peers:
+            waiter(ar.at[s, 0 : count - 1], ar_recv.at[s]).wait_recv()
         part = ar[s, 0]
         for i in range(1, count):
             part = part + ar[s, i]
@@ -366,8 +401,9 @@
     dskip_ref[...] = part[:, H : 2 * H]
     store_out(dalog_ref, dalog_hbm)
     store_out(dskip_ref, dskip_hbm)
-    for copy in sent:
-        copy.wait_send()
+    for s, (mine, count, peers) in enumerate(stages):
+        if peers:
+            waiter(ar.at[s, 0 : count - 1], ar_send.at[s]).wait_send()
     for copy in stored:
         copy.wait()
 
@@ -428,8 +464,10 @@
             pltpu.VMEM((T, HD), f32),
             pltpu.VMEM((16, HD), f32),
             pltpu.VMEM((8, HD), f32),
-            pltpu.VMEM((RING, K, 2 * N + 8, W), f32),
-            pltpu.VMEM((RING, K, 2 * N + 8, W), f32),
+            pltpu.VMEM((RING, K, 2 * N, W), f32),
+            pltpu.VMEM((RING, K, 2 * N, W), f32),
+            pltpu.VMEM((RING, 8, W), f32),
+            pltpu.VMEM((RING, 8, W), f32),
             pltpu.VMEM((K, 2, N + 8, W), f32),
             pltpu.VMEM((K, 2, N + 8, W), f32),
             pltpu.VMEM((K, 2, N + 8, W), f32),
@@ -440,18 +478,11 @@
             pltpu.VMEM((2, slots, 1, 128), f32),
             dma((6 + 2 * K,)),
             dma((5 + K,)),
-            dma((RING, K)),
-            dma((RING, K)),
-            dma((K, 2)),
-            dma((K, 2)),
-            dma((K, 2)),
-            dma((K, 2)),
-            dma((K, 2)),
-            dma((K, 2)),
-            dma((RING, K)),
-            dma((RING, K)),
-            dma((2, slots)),
-            dma((2, slots)),
+            *(dma((K,)) for _ in range(10)),
+            dma((1,)),
+            dma((1,)),
+            dma((2,)),
+            dma((2,)),
             pltpu.SemaphoreType.REGULAR,
         ],
         compiler_params=pltpu.CompilerParams(

time: 58.2 us -> 56.4 us (0.969)
  Pallas kernels: 57.4 us -> 55.6 us
    pallas_call x1, Pallas kernels: 55.4 us -> 53.7 us  [per_device(): pl.pallas_call(functools.partial(kernel, dims), out_shape=outs, in_specs=...]
where the time goes in v5:
time: 56.4 us; the launch traced here: 56.3 us
  Pallas kernels  55.6 us (99%)
  between operations  0.64 us (1%)
    pallas_call x1, Pallas kernels, per_device(): pl.pallas_call(functools.partial(kernel, dims), out_shape=outs, in_specs=...  53.7 us
    pallas_call x1, Pallas kernels, per_device(): pl.pallas_call(functools.partial(write_out, plan), out_shape=outs, in_spe...  1.92 us

profile of v5, /device:TPU:1, one launch (start us, length us, event | category | flops | bytes accessed | tf_op | source)
XLA Modules:
  0.0 56.3 jit_solution(9675328877908929905)
XLA Ops:
  0.6 53.7 %ssd_backward.1 = (bf16[128,2048]{1,0:T(8,128)(2,1)}, bf16[64,128]{1,0:T(8,128)(2,1)}, bf16[64,128]{1,0:T(8,128)(2,1)}, f32[32,128]{1,0:T(8,128)}, f32[1,32]{1,0:T(1,128)}, /*index=5*/f32[1,32]{1,0:T(1,128)}) custom-call(bf16[128,2048]{1,0:T(8,128)(2,1)} %bitcast.21, bf16[128,2048]{1,0:T(8,128)(2,1)} %bitcast.22, bf16[64,128]{1,0:T(8,128)(2,1)} %bitcast.23, ...), custom_call_target="tpu_custom_call" | custom-call | tf_op jit(solution)/shard_map/ssd_backward/pallas_call | solution.py:445
  54.4 1.9 %write_out.1 = (bf16[128,2048]{1,0:T(8,128)(2,1)}, bf16[64,128]{1,0:T(8,128)(2,1)}, bf16[64,128]{1,0:T(8,128)(2,1)}, f32[32,128]{1,0:T(8,128)}, f32[1,32]{1,0:T(1,128)}, /*index=5*/f32[1,32]{1,0:T(1,128)}) custom-call(bf16[128,2048]{1,0:T(8,128)(2,1)} %get-tuple-element.18.refs_0_, bf16[64,128]{1,0:T(8,128)(2,1)} %get-tuple-element.19.refs_1_, ...), custom_call_target="tpu_custom_call" | custom-call | tf_op jit(solution)/shard_map/write_out/pallas_call | solution.py:497

commit v6 on v5

--- a/solution.py
+++ b/solution.py
@@ -40,11 +40,10 @@
 def kernel(
     dims,
     x_hbm, g_hbm, bt_hbm, ct_hbm, dt_hbm, alog_hbm, skip_hbm, len_hbm,
-    dx_hbm, db_hbm, dc_hbm, dstep_hbm, dalog_hbm, dskip_hbm,
     dx_ref, db_ref, dc_ref, dstep_ref, dalog_ref, dskip_ref,
     x_ref, g_ref, bt_ref, ct_ref, dt_ref, alog_ref, skip_ref, len_ref,
     xh, gh, bd, z1, z2, rowv, vecs, sa, ra, st, rt, s1, r1, s2, r2, r3, sc, rc, ar,
-    load, store, sa_send, sa_recv, s1_send, r1_recv, s2_send, r2_recv, s3_send, r3_recv, sc_send, sc_recv, st_send, rt_recv, ar_send, ar_recv, known,
+    load, sa_send, sa_recv, s1_send, r1_recv, s2_send, r2_recv, s3_send, r3_recv, sc_send, sc_recv, st_send, rt_recv, ar_send, ar_recv, known,
 ):
     n_dp, n_ctx, n_z, T, H, D, N, DOCS = dims
     n_x = n_ctx // (n_z * RING)
@@ -173,14 +172,6 @@
         return pltpu.make_async_remote_copy(
             src_ref=ref, dst_ref=ref, send_sem=sem, recv_sem=sem, device_id=(dp, me), device_id_type=MESH
         )
-
-    stored = []
-
-    def store_out(src, dst):
-        copy = pltpu.make_async_copy(src, dst, store.at[len(stored)])
-        copy.start()
-        stored.append(copy)
-
 
     per = C // D
     row_k = lax.broadcasted_iota(jnp.int32, (8, H), 0)
@@ -347,7 +338,6 @@
 
         def remainder():
             dx_ref[:, at] = (bd[:, at] * z1_w + rowv[0:1, at] * g_ref[:, at].astype(f32)).astype(bf16)
-            store_out(dx_ref.at[:, at], dx_hbm.at[:, at])
             sums[2] = sums[2] + nt(hh, gp)
             sums[3] = sums[3] + nt(fh, xp)
 
@@ -388,8 +378,6 @@
             for piece in split(d_cum, 3):
                 d_log = d_log + nn(piece, tril)
             dstep_ref[...] = col_q / dt + d_log * rate_c
-            for src, dst in ((dc_ref, dc_hbm), (db_ref, db_hbm), (dstep_ref, dstep_hbm)):
-                store_out(src, dst)
             for ref, sem in sent:
                 waiter(ref, sem).wait_send()
         if peers:
@@ -399,28 +387,17 @@
             part = part + ar[s, i]
     dalog_ref[...] = part[:, :H]
     dskip_ref[...] = part[:, H : 2 * H]
-    store_out(dalog_ref, dalog_hbm)
-    store_out(dskip_ref, dskip_hbm)
     for s, (mine, count, peers) in enumerate(stages):
         if peers:
             waiter(ar.at[s, 0 : count - 1], ar_send.at[s]).wait_send()
-    for copy in stored:
+
+
+def write_out(count, *refs):
+    copies = [pltpu.make_async_copy(refs[i], refs[count + i], refs[-1].at[i]) for i in range(count)]
+    for copy in copies:
+        copy.start()
+    for copy in copies:
         copy.wait()
-
-
-def write_out(plan, *refs):
-    count = len(refs) // 3
-    sources, targets, places, loaded, stored = refs[:count], refs[count : 2 * count], refs[2 * count : 3 * count], *refs[-2:]
-    copies = []
-    for n, (i, at) in enumerate(plan):
-        load = pltpu.make_async_copy(sources[i].at[:, at], places[i].at[:, at], loaded.at[n])
-        copies.append((load, pltpu.make_async_copy(places[i].at[:, at], targets[i].at[:, at], stored.at[n])))
-        load.start()
-    for load, store in copies:
-        load.wait()
-        store.start()
-    for _, store in copies:
-        store.wait()
 
 
 def per_device(n_dp, n_ctx, n_z, inputs, b_proj, c_proj, step_sizes, a_log, skip_gain, doc_lengths, grad_out):
@@ -432,7 +409,7 @@
     n_x = n_ctx // (n_z * RING)
     slots = max(RING * n_dp * n_x, 2 * n_z)
     dims = (n_dp, n_ctx, n_z, T, H, D, N, DOCS)
-    hbm = pl.BlockSpec(memory_space=pltpu.HBM)
+    vmem, hbm = pl.BlockSpec(memory_space=pltpu.VMEM), pl.BlockSpec(memory_space=pltpu.HBM)
     dma = pltpu.SemaphoreType.DMA
     outs = (
         jax.ShapeDtypeStruct((T, HD), bf16),
@@ -446,9 +423,8 @@
         functools.partial(kernel, dims),
         out_shape=outs,
         in_specs=[hbm] * 8,
-        out_specs=(hbm,) * 6,
+        out_specs=(vmem,) * 6,
         scratch_shapes=[
-            *(pltpu.VMEM(o.shape, o.dtype) for o in outs),
             pltpu.VMEM((T, HD), bf16),
             pltpu.VMEM((T, HD), bf16),
             pltpu.VMEM((N, T), bf16),
@@ -477,7 +453,6 @@
             pltpu.VMEM((RING, K, 2 * N, W), f32),
             pltpu.VMEM((2, slots, 1, 128), f32),
             dma((6 + 2 * K,)),
-            dma((5 + K,)),
             *(dma((K,)) for _ in range(10)),
             dma((1,)),
             dma((1,)),
@@ -486,21 +461,25 @@
             pltpu.SemaphoreType.REGULAR,
         ],
         compiler_params=pltpu.CompilerParams(
-            collective_id=0, has_side_effects=True, vmem_limit_bytes=60 << 20
+            collective_id=0, has_side_effects=True, vmem_limit_bytes=40960 << 10
         ),
         name="ssd_backward",
     )(
-        inputs[0], grad_out[0], b_proj[0].T, c_proj[0].T, step_sizes[0],
-        a_log[None], skip_gain[None], doc_lengths,
+        *(
+            pltpu.with_memory_space_constraint(a, pltpu.HBM)
+            for a in (
+                inputs[0], grad_out[0], b_proj[0].T, c_proj[0].T, step_sizes[0],
+                a_log[None], skip_gain[None], doc_lengths,
+            )
+        )
     )
-    plan = [(0, slice(lo, lo + 512)) for lo in range(0, HD, 512)] + [(i, slice(None)) for i in range(1, len(outs))]
     dx, db, dc, dstep, dalog, dskip = pl.pallas_call(
-        functools.partial(write_out, plan),
+        functools.partial(write_out, len(outs)),
         out_shape=outs,
-        in_specs=[hbm] * 6,
+        in_specs=[vmem] * 6,
         out_specs=(hbm,) * 6,
-        scratch_shapes=[*(pltpu.VMEM(o.shape, o.dtype) for o in outs), dma((len(plan),)), dma((len(plan),))],
-        compiler_params=pltpu.CompilerParams(vmem_limit_bytes=60 << 20),
+        scratch_shapes=[dma((len(outs),))],
+        compiler_params=pltpu.CompilerParams(vmem_limit_bytes=1 << 20),
         name="write_out",
     )(*results)
     return dx[None], db.T[None], dc.T[None], dstep[None], dalog[0], dskip[0]

time: 56.4 us -> 54.7 us (0.970)
  Pallas kernels: 55.6 us -> 53.9 us
    pallas_call x1, Pallas kernels: 1.92 us -> 0.86 us  [per_device(): pl.pallas_call(functools.partial(write_out, len(outs)), out_shape=outs, i...]
    pallas_call x1, Pallas kernels: 53.7 us -> 53.1 us  [per_device(): pl.pallas_call(functools.partial(kernel, dims), out_shape=outs, in_specs=...]
where the time goes in v6:
time: 54.7 us; the launch traced here: 54.6 us
  Pallas kernels  53.9 us (99%)
  between operations  0.64 us (1%)
    pallas_call x1, Pallas kernels, per_device(): pl.pallas_call(functools.partial(kernel, dims), out_shape=outs, in_specs=...  53.1 us

profile of v6, /device:TPU:1, one launch (start us, length us, event | category | flops | bytes accessed | tf_op | source)
XLA Modules:
  0.0 54.6 jit_solution(12944004596681125451)
XLA Ops:
  0.6 53.1 %ssd_backward.1 = (bf16[128,2048]{1,0:T(8,128)(2,1)S(1)}, bf16[64,128]{1,0:T(8,128)(2,1)S(1)}, bf16[64,128]{1,0:T(8,128)(2,1)S(1)}, f32[32,128]{1,0:T(8,128)S(1)...) custom-call(bf16[128,2048]{1,0:T(8,128)(2,1)} %bitcast.21, bf16[128,2048]{1,0:T(8,128)(2,1)} %bitcast.22, ...), custom_call_target="tpu_custom_call" | custom-call | tf_op jit(solution)/shard_map/ssd_backward/pallas_call | solution.py:422
  53.7 0.9 %write_out.1 = (bf16[128,2048]{1,0:T(8,128)(2,1)}, bf16[64,128]{1,0:T(8,128)(2,1)}, bf16[64,128]{1,0:T(8,128)(2,1)}, f32[32,128]{1,0:T(8,128)}, f32[1,32]{1,0:T(1,128)}, /*index=5*/f32[1,32]{1,0:T(1,128)}) custom-call(bf16[128,2048]{1,0:T(8,128)(2,1)S(1)} %get-tuple-element.18.refs_0_, bf16[64,128]{1,0:T(8,128)(2,1)S(1)} %get-tuple-element.19.refs_1_, ...), custom_call_target="tpu_custom_call" | custom-call | tf_op jit(solution)/shard_map/write_out/pallas_call | solution.py:476

commit v7 on v6

--- a/solution.py
+++ b/solution.py
@@ -14,8 +14,10 @@
 RING = 4
 CHUNKS = 4
 ORDER = (
-    ("total", 0), ("total", 1), ("pair", 0), ("total", 2), ("pair", 1), ("total", 3), ("pair", 2), ("give", 0),
-    ("pair", 3), ("give", 1), ("give", 2), ("finish", 0), ("give", 3), ("finish", 1), ("finish", 2), ("finish", 3),
+    ("total", 0), ("total", 1, 0), ("pair", 0, 0), ("total", 1, 1), ("pair", 0, 1), ("total", 2, 0),
+    ("pair", 1, 0), ("total", 2, 1), ("pair", 1, 1), ("total", 3, 0), ("pair", 2, 0), ("total", 3, 1),
+    ("pair", 2, 1), ("give", 0, 0), ("give", 0, 1), ("pair", 3, 0), ("pair", 3, 1), ("give", 1),
+    ("give", 2), ("give", 3), ("finish", 0), ("finish", 1), ("finish", 2), ("finish", 3),
 )
 
 
@@ -212,9 +214,11 @@
                 send(st.at[q], rt.at[y], st_send.at[0], rt_recv.at[0], (dp, group * RING + q))
             sent.append((st.at[0 : RING - 1], st_send.at[0]))
             rt[y] = st[y]
-        for _, q in y_peers:
-            send(sa.at[q, k], ra.at[y, k], sa_send.at[k], sa_recv.at[k], (dp, group * RING + q))
-        sent.append((sa.at[0 : RING - 1, k], sa_send.at[k]))
+        for side in (0, 1):
+            half, i = slice(side * N, side * N + N), 2 * k + side
+            for _, q in y_peers:
+                send(sa.at[q, k, half, :], ra.at[y, k, half, :], sa_send.at[i], sa_recv.at[i], (dp, group * RING + q))
+            sent.append((sa.at[0 : RING - 1, k, half, :], sa_send.at[i]))
         ra[y, k] = sa[y, k]
         rowv[0:8, at] = nn(skip3, hot)[0:8]
         rowv[8:16, at] = jnp.broadcast_to(last_alpha, (8, C))
@@ -264,58 +268,60 @@
     def pulled(r, k):
         return ra[r, k, N : 2 * N, :]
 
-    def total(k):
-        if k == 0:
+    def total(k, sides=(0, 1)):
+        if k == 0 and 0 in sides:
             waiter(rt.at[0 : RING - 1], rt_recv.at[0]).wait_recv()
-        waiter(ra.at[0 : RING - 1, k], sa_recv.at[k]).wait_recv()
-        up, down = own(0, k), pulled(RING - 1, k)
         across = through_of(0, k)
         for i in range(1, RING):
-            j = RING - 1 - i
-            up = own(i, k) + through_of(i, k) * up
-            down = pulled(j, k) + through_of(j, k) * down
             across = across * through_of(i, k)
-        for side, value in ((0, up), (1, down)):
+        for side in sides:
+            waiter(ra.at[0 : RING - 1, k, side * N : side * N + N, :], sa_recv.at[2 * k + side]).wait_recv()
+            if side == 0:
+                value = own(0, k)
+                for i in range(1, RING):
+                    value = own(i, k) + through_of(i, k) * value
+            else:
+                value = pulled(RING - 1, k)
+                for i in range(RING - 2, -1, -1):
+                    value = pulled(i, k) + through_of(i, k) * value
             s1[k, side, 0:N, :] = value
             s1[k, side, N : N + 8, :] = jnp.broadcast_to(across, (8, W))
-            send(s1.at[k, side], r1.at[k, side], s1_send.at[k], r1_recv.at[k], z_near[side])
-        sent.append((s1.at[k], s1_send.at[k]))
-
-    def pair(k):
-        waiter(r1.at[k], r1_recv.at[k]).wait_recv()
-        for side in (0, 1):
+            i = 2 * k + side
+            send(s1.at[k, side], r1.at[k, side], s1_send.at[i], r1_recv.at[i], z_near[side])
+            sent.append((s1.at[k, side], s1_send.at[i]))
+
+    def pair(k, sides=(0, 1)):
+        for side in sides:
+            i = 2 * k + side
+            waiter(r1.at[k, side], r1_recv.at[i]).wait_recv()
             across = s1[k, side, N : N + 8, :]
             s2[k, side, 0:N, :] = s1[k, side, 0:N, :] + across[0:1] * r1[k, side, 0:N, :]
             s2[k, side, N : N + 8, :] = across * r1[k, side, N : N + 8, :]
-            send(s2.at[k, side, 0:N, :], r3.at[k, side], s3_send.at[k], r3_recv.at[k], z_far[side])
-            send(s2.at[k, side], r2.at[k, side], s2_send.at[k], r2_recv.at[k], z_near[side])
-        sent.append((r3.at[k], s3_send.at[k]))
-        sent.append((s2.at[k], s2_send.at[k]))
-
-    def give(k):
-        enters = []
-        waiter(r2.at[k], r2_recv.at[k]).wait_recv()
-        waiter(r3.at[k], r3_recv.at[k]).wait_recv()
-        for side in (0, 1):
-            enters.append(r2[k, side, 0:N, :] + r2[k, side, N : N + 1, :] * r3[k, side])
-        up, down = enters
-        for i in range(RING):
-            j = RING - 1 - i
-            sc[i, k, 0:N, :] = up
-            sc[j, k, N : 2 * N, :] = down
-            if i + 1 < RING:
-                up = own(i, k) + through_of(i, k) * up
-                down = pulled(j, k) + through_of(j, k) * down
-        for _, q in y_peers:
-            send(sc.at[q, k], rc.at[y, k], sc_send.at[k], sc_recv.at[k], (dp, group * RING + q))
-        sent.append((sc.at[0 : RING - 1, k], sc_send.at[k]))
-        rc[y, k] = sc[y, k]
+            send(s2.at[k, side, 0:N, :], r3.at[k, side], s3_send.at[i], r3_recv.at[i], z_far[side])
+            send(s2.at[k, side], r2.at[k, side], s2_send.at[i], r2_recv.at[i], z_near[side])
+            sent.append((r3.at[k, side], s3_send.at[i]))
+            sent.append((s2.at[k, side], s2_send.at[i]))
+
+    def give(k, sides=(0, 1)):
+        for side in sides:
+            half, n = slice(side * N, side * N + N), 2 * k + side
+            waiter(r2.at[k, side], r2_recv.at[n]).wait_recv()
+            waiter(r3.at[k, side], r3_recv.at[n]).wait_recv()
+            value = r2[k, side, 0:N, :] + r2[k, side, N : N + 1, :] * r3[k, side]
+            for i in range(RING) if side == 0 else range(RING - 1, -1, -1):
+                sc[i, k, half, :] = value
+                value = (own(i, k) if side == 0 else pulled(i, k)) + through_of(i, k) * value
+            for _, q in y_peers:
+                send(sc.at[q, k, half, :], rc.at[y, k, half, :], sc_send.at[n], sc_recv.at[n], (dp, group * RING + q))
+            sent.append((sc.at[0 : RING - 1, k, half, :], sc_send.at[n]))
+            rc[y, k, half, :] = sc[y, k, half, :]
 
     sums = [jnp.zeros((H, 2 * T), f32), jnp.zeros((H, 2 * T), f32), jnp.zeros((2 * N, 2 * T), f32), jnp.zeros((2 * N, 2 * T), f32), jnp.zeros((H, 8), f32)]
 
     def finish(k):
         at = slice(k * C, (k + 1) * C)
-        waiter(rc.at[0 : RING - 1, k], sc_recv.at[k]).wait_recv()
+        for side in (0, 1):
+            waiter(rc.at[0 : RING - 1, k, side * N : side * N + N, :], sc_recv.at[2 * k + side]).wait_recv()
         hot = one_hot(k, 1)
         state = jnp.concatenate([rc[q, k, 0:N, :] for q in range(RING)], axis=1)
         later = jnp.concatenate([rc[q, k, N : 2 * N, :] for q in range(RING)], axis=1)
@@ -348,8 +354,8 @@
 
     put_off = []
     steps = {"total": total, "pair": pair, "give": give, "finish": finish}
-    for name, k in ORDER:
-        steps[name](k)
+    for name, k, *sides in ORDER:
+        steps[name](k, *([sides] if sides else []))
 
     col_q = sums[0][:, :T] + sums[0][:, T:]
     row_q = sums[1][:, :T] + sums[1][:, T:]
@@ -361,7 +367,7 @@
     part = jnp.where(rows[:H] == cols[:H], d_alog, jnp.where(rows[:H] + H == cols[:H], d_skip, 0.0))
     part = jnp.sum(part, axis=0, keepdims=True)
 
-    stages = ((plane, n_plane, plane_peers), (line, n_line, line_peers))
+    stages = ((line, n_line, line_peers), (plane, n_plane, plane_peers))
     pl.semaphore_wait(known, len(x_peers) + len(core_peers))
     for s, (mine, count, peers) in enumerate(stages):
         ar[s, mine] = part
@@ -453,7 +459,7 @@
             pltpu.VMEM((RING, K, 2 * N, W), f32),
             pltpu.VMEM((2, slots, 1, 128), f32),
             dma((6 + 2 * K,)),
-            *(dma((K,)) for _ in range(10)),
+            *(dma((2 * K,)) for _ in range(10)),
             dma((1,)),
             dma((1,)),
             dma((2,)),

time: 54.7 us -> 53.3 us (0.974)
  Pallas kernels: 53.9 us -> 52.6 us
    pallas_call x1, Pallas kernels: 53.1 us -> 51.7 us  [per_device(): pl.pallas_call(functools.partial(kernel, dims), out_shape=outs, in_specs=...]
where the time goes in v7:
time: 53.3 us; the launch traced here: 53.2 us
  Pallas kernels  52.6 us (99%)
  between operations  0.64 us (1%)
    pallas_call x1, Pallas kernels, per_device(): pl.pallas_call(functools.partial(kernel, dims), out_shape=outs, in_specs=...  51.7 us

profile of v7, /device:TPU:1, one launch (start us, length us, event | category | flops | bytes accessed | tf_op | source)
XLA Modules:
  0.0 53.2 jit_solution(3929245524359833326)
XLA Ops:
  0.6 51.7 %ssd_backward.1 = (bf16[128,2048]{1,0:T(8,128)(2,1)S(1)}, bf16[64,128]{1,0:T(8,128)(2,1)S(1)}, bf16[64,128]{1,0:T(8,128)(2,1)S(1)}, f32[32,128]{1,0:T(8,128)S(1)...) custom-call(bf16[128,2048]{1,0:T(8,128)(2,1)} %bitcast.21, bf16[128,2048]{1,0:T(8,128)(2,1)} %bitcast.22, ...), custom_call_target="tpu_custom_call" | custom-call | tf_op jit(solution)/shard_map/ssd_backward/pallas_call | solution.py:428
  52.4 0.9 %write_out.1 = (bf16[128,2048]{1,0:T(8,128)(2,1)}, bf16[64,128]{1,0:T(8,128)(2,1)}, bf16[64,128]{1,0:T(8,128)(2,1)}, f32[32,128]{1,0:T(8,128)}, f32[1,32]{1,0:T(1,128)}, /*index=5*/f32[1,32]{1,0:T(1,128)}) custom-call(bf16[128,2048]{1,0:T(8,128)(2,1)S(1)} %get-tuple-element.18.refs_0_, bf16[64,128]{1,0:T(8,128)(2,1)S(1)} %get-tuple-element.19.refs_1_, ...), custom_call_target="tpu_custom_call" | custom-call | tf_op jit(solution)/shard_map/write_out/pallas_call | solution.py:482

commit v8 on v7

--- a/solution.py
+++ b/solution.py
@@ -94,9 +94,8 @@
     for b in range(1, n_core):
         core_peers.append((xlo * n_core + (core + b) % n_core, me))
     barrier = pltpu.get_barrier_semaphore()
-    greeted = [(dp, group * RING + q) for _, q in y_peers]
-    greeted += z_near + z_far + x_peers + core_peers
-    greeted += [(dp, (xhi * n_z + (z + d) % n_z) * RING + y) for d in range(1, n_z)]
+    greeted = [(dp, (xhi * n_z + (z + d) % n_z) * RING + y) for d in sorted(range(1, n_z), key=lambda d: -far(d, n_z))]
+    greeted += z_far + z_near + [(dp, group * RING + q) for _, q in y_peers] + x_peers + core_peers
     for target in greeted:
         pl.semaphore_signal(barrier, inc=1, device_id=target, device_id_type=MESH)
     for copy in loads[small + 2 :]:
@@ -320,25 +319,26 @@
 
     def finish(k):
         at = slice(k * C, (k + 1) * C)
-        for side in (0, 1):
-            waiter(rc.at[0 : RING - 1, k, side * N : side * N + N, :], sc_recv.at[2 * k + side]).wait_recv()
         hot = one_hot(k, 1)
+        waiter(rc.at[0 : RING - 1, k, 0:N, :], sc_recv.at[2 * k]).wait_recv()
         state = jnp.concatenate([rc[q, k, 0:N, :] for q in range(RING)], axis=1)
-        later = jnp.concatenate([rc[q, k, N : 2 * N, :] for q in range(RING)], axis=1)
+        hh = jnp.concatenate(split(state, 2), axis=0)
+        gp, xp = gh[:, at], xh[:, at]
+        z2_w = z2[:, at] + nn(lc, hh)
+        p2 = z2_w * (gp[:T].astype(f32) + gp[T:].astype(f32))
+        sums[1] = sums[1] + nt(hot, jnp.concatenate(split(p2, 2), axis=0))
         mine = jnp.concatenate([sa[q, k, 0:N, :] for q in range(RING)], axis=1)
         last_alpha = rowv[8:9, at]
-        leaving = jnp.sum(later * (mine + last_alpha * through_flag * state), axis=0, keepdims=True)
+        mine = mine + last_alpha * through_flag * state
+        waiter(rc.at[0 : RING - 1, k, N : 2 * N, :], sc_recv.at[2 * k + 1]).wait_recv()
+        later = jnp.concatenate([rc[q, k, N : 2 * N, :] for q in range(RING)], axis=1)
+        leaving = jnp.sum(later * mine, axis=0, keepdims=True)
         first_row = lax.broadcasted_iota(jnp.int32, (8, C), 0) == 0
         vec = jnp.where(first_row, leaving, vecs[:, at])
-        hh = jnp.concatenate(split(state, 2), axis=0)
         fh = jnp.concatenate(split(later * last_alpha, 2), axis=0)
         z1_w = z1[:, at] + nn(eb, fh)
-        z2_w = z2[:, at] + nn(lc, hh)
-        gp, xp = gh[:, at], xh[:, at]
         p1 = z1_w * (xp[:T].astype(f32) + xp[T:].astype(f32))
-        p2 = z2_w * (gp[:T].astype(f32) + gp[T:].astype(f32))
         sums[0] = sums[0] + nt(hot, jnp.concatenate(split(p1, 2), axis=0))
-        sums[1] = sums[1] + nt(hot, jnp.concatenate(split(p2, 2), axis=0))
         for piece in split(vec, 3):
             sums[4] = sums[4] + nt(hot, piece)
 

time: 53.3 us -> 53.2 us (level)
  no operation moved by 1% of the time
where the time goes in v8:
time: 53.2 us; the launch traced here: 53.1 us
  Pallas kernels  52.4 us (98%)
  between operations  0.64 us (1%)
    pallas_call x1, Pallas kernels, per_device(): pl.pallas_call(functools.partial(kernel, dims), out_shape=outs, in_specs=...  51.6 us

profile of v8, /device:TPU:1, one launch (start us, length us, event | category | flops | bytes accessed | tf_op | source)
XLA Modules:
  0.0 53.1 jit_solution(5699606707100262326)
XLA Ops:
  0.6 51.6 %ssd_backward.1 = (bf16[128,2048]{1,0:T(8,128)(2,1)S(1)}, bf16[64,128]{1,0:T(8,128)(2,1)S(1)}, bf16[64,128]{1,0:T(8,128)(2,1)S(1)}, f32[32,128]{1,0:T(8,128)S(1)...) custom-call(bf16[128,2048]{1,0:T(8,128)(2,1)} %bitcast.21, bf16[128,2048]{1,0:T(8,128)(2,1)} %bitcast.22, ...), custom_call_target="tpu_custom_call" | custom-call | tf_op jit(solution)/shard_map/ssd_backward/pallas_call | solution.py:428
  52.2 0.9 %write_out.1 = (bf16[128,2048]{1,0:T(8,128)(2,1)}, bf16[64,128]{1,0:T(8,128)(2,1)}, bf16[64,128]{1,0:T(8,128)(2,1)}, f32[32,128]{1,0:T(8,128)}, f32[1,32]{1,0:T(1,128)}, /*index=5*/f32[1,32]{1,0:T(1,128)}) custom-call(bf16[128,2048]{1,0:T(8,128)(2,1)S(1)} %get-tuple-element.18.refs_0_, bf16[64,128]{1,0:T(8,128)(2,1)S(1)} %get-tuple-element.19.refs_1_, ...), custom_call_target="tpu_custom_call" | custom-call | tf_op jit(solution)/shard_map/write_out/pallas_call | solution.py:482
